TPU v7x, 256 devices: a whole 4x4x8 slice. The times are simulated.
256 devices in a mesh: seq: 64 (over y_hi, x, z), tensor: 4 (over y_lo, core).
Axes of the slice: x: 4, y: 4 (y_hi: 2, y_lo: 2; y = y_hi * 2 + y_lo), z: 8, core: 2. Of those that a mesh axis runs over, the one named last changes fastest.
Arguments:
- latents: bfloat16 [8192, 2560], P('seq'), may hold values from -6 to 6
- levels: int32 [64], P('seq'), may hold values from 0 to 999
- head_slot: int32 [1], replicated, may hold values from 0 to 63
- fresh_noise: bfloat16 [128, 2560], P(None, 'tensor'), may hold values from -6 to 6
- ada_weight: bfloat16 [256, 3, 2560], P(None, None, 'tensor'), may hold values from -0.375 to 0.375
- qkv_weight: bfloat16 [2560, 3, 1536], P(None, None, 'tensor'), may hold values from -0.125 to 0.125
- q_gain: float32 [128], replicated, may hold values from 0.5 to 2.5
- k_gain: float32 [128], replicated, may hold values from 0.5 to 2.5
- out_weight: bfloat16 [1536, 2560], P('tensor'), may hold values from -0.15625 to 0.15625
Outputs:
- window: bfloat16 [8192, 2560], P('seq', 'tensor')
- clean: bfloat16 [128, 2560], P('seq', 'tensor')
All inputs are finite; a program needn't handle non-finite values.
Results may differ from a plain program's by a relative error of at most 0.0053.
Values may be sent and summed in bfloat16 or wider, within the bound.
No kernel may reach another device: no remote copies, remote signals or barrier semaphores. Data moves between devices by JAX's collectives and lax.ppermute only.
A program may use at most 64 MiB of HBM per device.

v0:
```python
import math

import jax
import jax.numpy as jnp
from jax import lax
from jax.sharding import PartitionSpec as P


def spread(shard, axis, root):
    mine = lax.axis_index(axis) == root
    return lax.psum(jnp.where(mine, shard, jnp.zeros_like(shard)), axis)


def modulation_part(levels, ada_weight):
    embed_width = ada_weight.shape[0]
    half_width = embed_width // 2
    frequency = jnp.exp(-math.log(10000.0) * jnp.arange(half_width, dtype=jnp.float32) / half_width)
    angles = levels.astype(jnp.float32)[:, None] * frequency[None, :]
    embedding = jax.nn.silu(jnp.concatenate([jnp.cos(angles), jnp.sin(angles)], axis=1)).astype(
        jnp.bfloat16
    )
    flat = jnp.dot(
        embedding, ada_weight.reshape(embed_width, -1), preferred_element_type=jnp.float32
    )
    return flat.reshape(3, -1)


def modulate(states, offset_terms, scale_terms):
    average = jnp.mean(states, axis=-1, keepdims=True)
    centered = states - average
    variance = jnp.mean(centered * centered, axis=-1, keepdims=True)
    normed = centered * lax.rsqrt(variance + 1e-06)
    return (normed * (1.0 + scale_terms) + offset_terms).astype(jnp.bfloat16)


def rms_scaled(matrix, gain_vector, factor):
    power = jnp.mean(matrix * matrix, axis=-1, keepdims=True)
    return (matrix * lax.rsqrt(power + 1e-06) * gain_vector * factor).astype(jnp.bfloat16)


def project(hidden, qkv_weight, q_gain, k_gain):
    head_size = q_gain.shape[0]
    projected_all = jnp.dot(
        hidden, qkv_weight.reshape(qkv_weight.shape[0], -1), preferred_element_type=jnp.float32
    )
    projected_all = projected_all.reshape(hidden.shape[0], 3, -1, head_size)
    queries = rms_scaled(projected_all[:, 0], q_gain, 1.0 / math.sqrt(head_size))
    keys = rms_scaled(projected_all[:, 1], k_gain, 1.0)
    values = projected_all[:, 2].astype(jnp.bfloat16)
    return (queries, keys, values)


def attend(queries, query_rank, keys, values, oldest, block_rows, block_count):
    row_count = queries.shape[0]
    head_count = queries.shape[1]
    head_size = queries.shape[2]
    initial = (
        jnp.zeros((head_count, row_count), jnp.float32),
        jnp.zeros((row_count, head_count, head_size), jnp.float32),
    )
    key_piece = lax.all_gather(keys, "seq", axis=0, tiled=True)
    value_piece = lax.all_gather(values, "seq", axis=0, tiled=True)
    key_count = key_piece.shape[0]
    key_index = jnp.arange(key_count, dtype=jnp.int32) // block_rows
    key_rank = (key_index - oldest) % block_count
    visible = key_rank[None, :] <= query_rank[:, None]

    def update_state(state_old):
        scores = jnp.einsum("qhd,khd->hqk", queries, key_piece, preferred_element_type=jnp.float32)
        weights = jnp.where(visible[None], jnp.exp(scores), 0.0)
        running_sum = jnp.sum(weights, axis=-1)
        weighted = jnp.einsum(
            "hqk,khd->qhd",
            weights.astype(jnp.bfloat16),
            value_piece,
            preferred_element_type=jnp.float32,
        )
        return (running_sum, weighted)

    def keep_state(state_old):
        return state_old

    finished = lax.cond(jnp.any(visible), update_state, keep_state, initial)
    return (finished[1] / finished[0].T[..., None]).astype(jnp.bfloat16)


def local(
    latents, levels, head_slot, fresh_noise, ada_weight, qkv_weight, q_gain, k_gain, out_weight
):
    frames = latents.shape[0]
    seq_devices = lax.axis_size("seq")
    position = lax.axis_index("seq")
    oldest = head_slot[0]
    own_rank = (position - oldest) % seq_devices
    local_terms = modulation_part(levels, ada_weight)
    modulations = lax.all_gather(local_terms, "tensor", axis=1, tiled=True)
    states = latents.astype(jnp.float32)
    hidden = modulate(states, modulations[0][None], modulations[1][None])
    queries, keys, values = project(hidden, qkv_weight, q_gain, k_gain)
    row_rank = jnp.full((frames,), own_rank, jnp.int32)
    attended = attend(queries, row_rank, keys, values, oldest, frames, seq_devices).reshape(
        frames, -1
    )
    partial_sum = jnp.dot(attended, out_weight, preferred_element_type=jnp.float32)
    width_local = fresh_noise.shape[1]
    first_column = lax.axis_index("tensor") * width_local
    summed = lax.psum(partial_sum, "tensor")
    projected = lax.dynamic_slice_in_dim(summed, first_column, width_local, 1)
    own_states = lax.dynamic_slice_in_dim(states, first_column, width_local, 1)
    own_gate = lax.dynamic_slice_in_dim(modulations[2], first_column, width_local, 0)
    updated = (own_states + own_gate[None, :] * projected).astype(jnp.bfloat16)
    leaving_block = spread(updated, "seq", oldest)
    clean_rows = frames // seq_devices
    clean = lax.dynamic_slice_in_dim(leaving_block, position * clean_rows, clean_rows, 0)
    window = jnp.where(own_rank == 0, fresh_noise, updated)
    return (window, clean)


def solution(mesh):
    return jax.shard_map(
        local,
        mesh=mesh,
        in_specs=(
            P("seq", None),
            P("seq"),
            P(),
            P(None, "tensor"),
            P(None, None, "tensor"),
            P(None, None, "tensor"),
            P(),
            P(),
            P("tensor", None),
        ),
        out_specs=(P("seq", "tensor"), P("seq", "tensor")),
        check_vma=False,
    )
```

profile of v0, /device:TPU:8, one launch (start us, length us, event | category | flops | bytes accessed | tf_op | source)
XLA Modules:
  0.0 966.1 jit_solution(4467069962074013815)
XLA Ops:
  7.2 0.0 all-gather.4.cloned.1.call-start
  7.2 9.0 copy.15
  17.1 2.3 copy.14
  19.3 1.6 fusion.5
  20.9 5.4 all_gather.9
  26.3 0.1 fusion.20
  26.4 0.2 convert_reduce_fusion
  26.6 0.3 multiply_reduce_fusion
  27.0 4.5 fusion.8
  31.5 0.8 multiply_convert_fusion
  32.3 0.0 all-gather.4.cloned.1.call-update
  32.3 0.0 all-gather.6.cloned.1.call-start
  32.4 0.7 slice.46
  33.0 0.0 all-gather.6.cloned.1.call-update
  33.1 0.0 all-reduce.3.cloned.1.call-start
  33.8 1.8 broadcast_reduce_fusion
  36.3 119.0 %all-gather.4.cloned.1.call-done = bf16[8192,3,128]{0,2,1:T(8,128)(2,1)} async-done(((bf16[128,3,128]{0,2,1:T(8,128)(2,1)}), bf16[8192,3,128]{0,2,1:T(8,128)(2,1)}) %all-gather.4.cloned.1.call-update) | async-done | bytes 6291472 | tf_op jit(solution)/shard_map/all_gather | solution.py:61
  155.3 122.6 %all-gather.6.cloned.1.call-done = bf16[8192,1,3,128]{0,3,2,1:T(8,128)(2,1)} async-done(((bf16[128,1,3,128]{0,3,2,1:T(8,128)(2,1)}), bf16[8192,1,3,128]{0,3,2,1:T(8,128)(2,1)}) %all-gather.6.cloned.1.call-update) | async-done | bytes 6291472 | tf_op jit(solution)/shard_map/all_gather | solution.py:62
  277.9 0.4 le.10
  278.3 8.5 conditional.1
  278.3 6.5 fusion.24
  284.8 1.8 fusion.2
  286.6 0.1 copy.26
  286.8 1.6 fusion.25
  288.4 0.0 all-reduce.5.cloned.1.call-start
  288.5 1.2 convert_element_type.37
  289.7 46.6 %all-reduce.3.cloned.1.call-done = f32[128,2560]{1,0:T(8,128)} async-done(((f32[128,2560]{1,0:T(8,128)}), f32[128,2560]{1,0:T(8,128)}) %all-reduce.3.cloned.1.call-update) | async-done | bytes 1310736 | tf_op jit(solution)/shard_map/psum | solution.py:107
  336.3 1.8 broadcast_select_fusion
  338.1 0.0 all-reduce.5.cloned.1.call-update
  338.1 0.7 broadcast_select_fusion.1
  338.8 619.5 %all-reduce.5.cloned.1.call-done = bf16[128,640]{1,0:T(8,128)(2,1)} async-done(((bf16[128,640]{1,0:T(8,128)(2,1)}), bf16[128,640]{1,0:T(8,128)(2,1)}) %all-reduce.5.cloned.1.call-update) | async-done | bytes 163856 | tf_op jit(solution)/shard_map/psum | solution.py:11
  958.3 1.3 constant_dynamic-slice_fusion
  (25 shorter events, 0.3 us)
Async XLA Ops:
  7.2 279.6 %copy-start = (bf16[384,2560]{1,0:T(8,128)(2,1)S(1)}, bf16[384,2560]{1,0:T(8,128)(2,1)}, u32[]{:S(2)}) copy-start(bf16[384,2560]{1,0:T(8,128)(2,1)} %param.19) | copy-start | bytes 5898244
  7.2 148.1 %all-gather.4.cloned.1.call-start = ((), (), s32[]{:S(2)}) async-start(), calls=%async_computation | async-start | bytes 6389760 | tf_op jit(solution)/shard_map/all_gather | solution.py:61
  16.2 10.2 %copy-start.2 = (bf16[128,2560]{1,0:T(8,128)(2,1)S(1)}, bf16[128,2560]{1,0:T(8,128)(2,1)}, u32[]{:S(2)}) copy-start(bf16[128,2560]{1,0:T(8,128)(2,1)} %param.11) | copy-start | bytes 1966084
  26.9 4.6 copy-start.4
  26.9 4.6 copy-start.5
  32.3 245.5 %all-gather.6.cloned.1.call-start = ((), (), s32[]{:S(2)}) async-start(), calls=%async_computation.3 | async-start | bytes 6389760 | tf_op jit(solution)/shard_map/all_gather | solution.py:62
  33.1 303.3 %all-reduce.3.cloned.1.call-start = ((), (), s32[]{:S(2)}) async-start(), calls=%async_computation.1 | async-start | bytes 2621440 | tf_op jit(solution)/shard_map/psum | solution.py:107
  278.3 6.5 copy-start.1
  288.4 49.7 %copy-start.3 = (bf16[128,640]{1,0:T(8,128)(2,1)S(1)}, bf16[128,640]{1,0:T(8,128)(2,1)}, u32[]{:S(2)}) copy-start(bf16[128,640]{1,0:T(8,128)(2,1)} %param.14) | copy-start | bytes 491524
  288.4 669.9 %all-reduce.5.cloned.1.call-start = ((), (), s32[]{:S(2)}) async-start(), calls=%async_computation.2 | async-start | bytes 327680 | tf_op jit(solution)/shard_map/psum | solution.py:11
Sparse Core Ops, SparseCore 0:
  32.4 122.7 all-gather.3
  158.7 119.1 all-gather.5
  288.5 47.7 all-reduce.2
  338.8 619.4 all-reduce.4
where the time goes:
time: 967 us; the launch traced here: 966 us
  waiting for transfers between devices  908 us (94%)
  between operations  16 us (2%)
  matrix products  15.9 us (2%)
  local copies, waits for them, and re-layouts  13.8 us (1%)
    psum x1, waiting for transfers between devices, spread(): return lax.psum(jnp.where(mine, shard, jnp.zeros_like(shard)), axis)  619 us
    all_gather x1, waiting for transfers between devices, attend(): value_piece = lax.all_gather(values, 'seq', axis=0, tiled=True)  123 us
    all_gather x1, waiting for transfers between devices, attend(): key_piece = lax.all_gather(keys, 'seq', axis=0, tiled=True)  119 us
    psum x1, waiting for transfers between devices, local(): summed = lax.psum(partial_sum, 'tensor')  46.6 us
  transfers between devices with their start and end apart: 4, of which 4 were waited for; matrix products, arithmetic and copies ran while one was open for 0% of the time, Pallas kernels for 0%

commit v1 on v0

v1 whole, which is shorter than its diff:
```python
import functools
import math

import jax
import jax.numpy as jnp
from jax import lax
from jax.experimental import pallas as pl
from jax.experimental.pallas import tpu as pltpu
from jax.sharding import Mesh
from jax.sharding import PartitionSpec as P

F32 = jnp.float32
BF16 = jnp.bfloat16
COLS = 8
LINE = 8
BLOCKS = COLS * LINE
ROWS = 128
HD = 128
NH = 3
D = 2560
QW = D // 4
QROWS = NH * ROWS
EXTRA = 144
SEND = QROWS + EXTRA
BACK = QROWS + 16
OUTROWS = ROWS + 16


def vmem(n):
    return [pl.BlockSpec(memory_space=pltpu.VMEM)] * n


def smem():
    return pl.BlockSpec(memory_space=pltpu.SMEM)


def params(mib=48):
    return pltpu.CompilerParams(vmem_limit_bytes=mib << 20)


def dot(a, b):
    return jnp.dot(a, b, preferred_element_type=F32)


def dot_t(a, b):
    return lax.dot_general(a, b, (((1,), (1,)), ((), ())), preferred_element_type=F32)


def modulation_kernel(level_ref, ada_ref, out_ref):
    half = 128
    index = lax.broadcasted_iota(jnp.int32, (16, 2 * half), 1)
    place = jnp.where(index < half, index, index - half).astype(F32)
    frequency = jnp.exp(-math.log(10000.0) * place / half)
    angle = level_ref[0].astype(F32) * frequency
    wave = jnp.where(index < half, jnp.cos(angle), jnp.sin(angle))
    embedding = (wave * (1.0 / (1.0 + jnp.exp(-wave)))).astype(BF16)
    for j in range(3):
        row = dot(embedding, ada_ref[j])[0:1]
        out_ref[pl.ds(j, 1), :] = row


def modulation(levels, ada):
    return pl.pallas_call(
        modulation_kernel,
        out_shape=jax.ShapeDtypeStruct((8, QW), F32),
        in_specs=[smem()] + vmem(1),
        out_specs=vmem(1)[0],
        compiler_params=params(16),
        name="modulation",
    )(levels, ada)


def rms_rounded(matrix, gain, factor):
    power = jnp.mean(matrix * matrix, axis=-1, keepdims=True)
    return (matrix * lax.rsqrt(power + 1e-06) * gain * factor).astype(BF16)


def kv_kernel(lat_ref, mod_ref, w_ref, gain_ref, hidden_ref, kv_ref):
    step = pl.program_id(0)

    @pl.when(step == 0)
    def _():
        states = lat_ref[...].astype(F32)
        average = jnp.mean(states, axis=-1, keepdims=True)
        centered = states - average
        variance = jnp.mean(centered * centered, axis=-1, keepdims=True)
        normed = centered * lax.rsqrt(variance + 1e-06)
        for t in range(4):
            piece = normed[:, t * QW : (t + 1) * QW]
            shift = mod_ref[t, 0:1, :]
            scale = mod_ref[t, 1:2, :]
            hidden_ref[:, t * QW : (t + 1) * QW] = (piece * (1.0 + scale) + shift).astype(BF16)

    out = dot(hidden_ref[...], w_ref[0])

    @pl.when(step == 0)
    def _():
        for h in range(NH):
            kv_ref[h * ROWS : (h + 1) * ROWS, :] = rms_rounded(
                out[:, h * HD : (h + 1) * HD], gain_ref[...], 1.0
            )

    @pl.when(step == 1)
    def _():
        for h in range(NH):
            kv_ref[QROWS + h * ROWS : QROWS + (h + 1) * ROWS, :] = out[
                :, h * HD : (h + 1) * HD
            ].astype(BF16)


def keys_values(latents, mods, w, k_gain):
    full = lambda *shape: pl.BlockSpec(shape, lambda i: (0,) * len(shape))
    return pl.pallas_call(
        kv_kernel,
        grid=(2,),
        out_shape=(
            jax.ShapeDtypeStruct((ROWS, D), BF16),
            jax.ShapeDtypeStruct((2 * QROWS, HD), BF16),
        ),
        in_specs=[
            full(ROWS, D),
            full(4, 8, QW),
            pl.BlockSpec((1, D, QROWS), lambda i: (i + 1, 0, 0)),
            full(1, HD),
        ],
        out_specs=(full(ROWS, D), full(2 * QROWS, HD)),
        compiler_params=params(),
        name="keys_values",
    )(latents, mods, w, k_gain)


def query_kernel(scal_ref, hidden_ref, w_ref, gain_ref, kv_ref, lat_ref, mod_ref, out_ref):
    out = dot(hidden_ref[...], w_ref[0])
    queries = []
    for h in range(NH):
        q = rms_rounded(out[:, h * HD : (h + 1) * HD], gain_ref[...], 1.0 / math.sqrt(HD))
        queries.append(q)
        for c in range(COLS):
            out_ref[c, h * ROWS : (h + 1) * ROWS, :] = q
    for h in range(NH):
        keys = kv_ref[h * ROWS : (h + 1) * ROWS, :]
        values = kv_ref[QROWS + h * ROWS : QROWS + (h + 1) * ROWS, :]
        weights = jnp.exp(dot_t(queries[h], keys))
        total = jnp.sum(weights, axis=-1, keepdims=True)
        attended = (dot(weights.astype(BF16), values) / total).astype(BF16)
        for c in range(COLS):
            out_ref[c, QROWS + h * 16 : QROWS + (h + 1) * 16, :] = attended[c * 16 : (c + 1) * 16]
    first = pl.multiple_of(scal_ref[3] * QW, 128)
    for k in range(5):
        piece = lat_ref[:, pl.ds(first + k * 128, 128)]
        for c in range(COLS):
            at = QROWS + (NH + k) * 16
            out_ref[c, at : at + 16, :] = piece[c * 16 : (c + 1) * 16]
    rows = [mod_ref[2:3, k * 128 : (k + 1) * 128] for k in range(5)]
    high = [row.astype(BF16).astype(F32) for row in rows]
    low = [row - top for row, top in zip(rows, high)]
    gate = jnp.concatenate(high + low + [jnp.zeros((6, 128), F32)], axis=0).astype(BF16)
    for c in range(COLS):
        out_ref[c, QROWS + 128 : SEND, :] = gate


def query_parts(scal, hidden, w, q_gain, kv, latents, mod):
    full = lambda *shape: pl.BlockSpec(shape, lambda i: (0,) * len(shape))
    return pl.pallas_call(
        query_kernel,
        grid=(1,),
        out_shape=jax.ShapeDtypeStruct((COLS, SEND, HD), BF16),
        in_specs=[
            smem(),
            full(ROWS, D),
            pl.BlockSpec((1, D, QROWS), lambda i: (0, 0, 0)),
            full(1, HD),
            full(2 * QROWS, HD),
            full(ROWS, D),
            full(8, QW),
        ],
        out_specs=full(COLS, SEND, HD),
        compiler_params=params(),
        name="queries",
    )(scal, hidden, w, q_gain, kv, latents, mod)


def attention_kernel(scal_ref, q_ref, kv_ref, out_ref):
    column, line, oldest = scal_ref[0], scal_ref[1], scal_ref[2]
    part = 4
    key_block = lax.broadcasted_iota(jnp.int32, (1, LINE * ROWS), 1) // ROWS
    key_rank = (column * LINE + key_block - oldest) & (BLOCKS - 1)
    lane = lax.broadcasted_iota(jnp.int32, (ROWS, 128), 1)
    row16 = lax.broadcasted_iota(jnp.int32, (16, 128), 0)
    for first in range(0, COLS, part):
        query_block = first + lax.broadcasted_iota(jnp.int32, (part * ROWS, 1), 0) // ROWS
        query_rank = (query_block * LINE + line - oldest) & (BLOCKS - 1)
        seen = key_rank <= query_rank
        totals = []
        for h in range(NH):
            q = q_ref[first : first + part, h * ROWS : (h + 1) * ROWS, :].reshape(part * ROWS, HD)
            keys = kv_ref[:, h * ROWS : (h + 1) * ROWS, :].reshape(LINE * ROWS, HD)
            values = kv_ref[:, QROWS + h * ROWS : QROWS + (h + 1) * ROWS, :].reshape(
                LINE * ROWS, HD
            )
            weights = jnp.where(seen, jnp.exp(dot_t(q, keys)), 0.0)
            totals.append(jnp.sum(weights, axis=-1, keepdims=True))
            products = dot(weights.astype(BF16), values).astype(BF16)
            for b in range(part):
                out_ref[first + b, h * ROWS : (h + 1) * ROWS, :] = products[
                    b * ROWS : (b + 1) * ROWS
                ]
        for b in range(part):
            tile = jnp.zeros((ROWS, 128), F32)
            for h in range(NH):
                total = totals[h][b * ROWS : (b + 1) * ROWS]
                tile = jnp.where((lane == h) | (lane == h + NH), total, tile)
            tile = tile.T[0:16]
            high = tile.astype(BF16).astype(F32)
            out_ref[first + b, QROWS:BACK, :] = jnp.where(row16 < NH, high, tile - high).astype(
                BF16
            )


def partial_attention(scal, queries, kv):
    return pl.pallas_call(
        attention_kernel,
        out_shape=jax.ShapeDtypeStruct((COLS, BACK, HD), BF16),
        in_specs=[smem()] + vmem(2),
        out_specs=vmem(1)[0],
        compiler_params=params(),
        name="attention",
    )(scal, queries, kv)


def output_kernel(back_ref, leaving_ref, w_ref, out_ref, held_ref):
    sums = back_ref[0].astype(F32)
    for c in range(1, COLS):
        sums = sums + back_ref[c].astype(F32)
    tile = jnp.concatenate([sums[QROWS:BACK], jnp.zeros((ROWS - 16, 128), F32)], axis=0).T
    for h in range(NH):
        total = tile[:, h : h + 1] + tile[:, h + NH : h + NH + 1]
        held_ref[0:ROWS, h * HD : (h + 1) * HD] = (sums[h * ROWS : (h + 1) * ROWS] / total).astype(
            BF16
        )
        held_ref[ROWS:OUTROWS, h * HD : (h + 1) * HD] = jnp.concatenate(
            [leaving_ref[2 * h : 2 * h + 2, :].astype(F32), jnp.zeros((14, HD), F32)], axis=0
        ).astype(BF16)
    for t in range(4):
        out_ref[t] = dot(held_ref[...], w_ref[:, t * QW : (t + 1) * QW]).astype(BF16)


def output_parts(back, leaving, w):
    return pl.pallas_call(
        output_kernel,
        out_shape=jax.ShapeDtypeStruct((4, OUTROWS, QW), BF16),
        in_specs=vmem(3),
        out_specs=vmem(1)[0],
        scratch_shapes=[pltpu.VMEM((OUTROWS, QROWS), BF16)],
        compiler_params=params(),
        name="output",
    )(back, leaving, w)


def final_kernel(scal_ref, parts_ref, lat_ref, mod_ref, leaving_ref, fresh_ref, window_ref, clean_ref):
    projected = parts_ref[0].astype(F32)
    for t in range(1, 4):
        projected = projected + parts_ref[t].astype(F32)
    first = pl.multiple_of(scal_ref[3] * QW, 128)
    own = scal_ref[0] * LINE + scal_ref[1] == scal_ref[2]
    leaving = leaving_ref[...].astype(F32)
    for k in range(5):
        at = slice(k * 128, (k + 1) * 128)
        states = lat_ref[:, pl.ds(first + k * 128, 128)].astype(F32)
        updated = (states + mod_ref[2:3, at] * projected[0:ROWS, at]).astype(BF16)
        window_ref[:, at] = jnp.where(own, fresh_ref[:, at], updated)
        gate = leaving[16 + k : 17 + k] + leaving[21 + k : 22 + k]
        old = leaving[2 * (NH + k) : 2 * (NH + k) + 2]
        clean_ref[:, at] = (old + gate * projected[ROWS : ROWS + 2, at]).astype(BF16)


def finish(scal, parts, latents, mod, leaving, fresh):
    return pl.pallas_call(
        final_kernel,
        out_shape=(
            jax.ShapeDtypeStruct((ROWS, QW), BF16),
            jax.ShapeDtypeStruct((2, QW), BF16),
        ),
        in_specs=[smem()] + vmem(5),
        out_specs=tuple(vmem(2)),
        compiler_params=params(),
        name="finish",
    )(scal, parts, latents, mod, leaving, fresh)


def local(
    latents, levels, head_slot, fresh_noise, ada_weight, qkv_weight, q_gain, k_gain, out_weight
):
    columns, line, tensor = ("yh", "x"), "z", ("yl", "core")
    oldest = head_slot[0]
    scal = jnp.stack(
        [lax.axis_index(columns), lax.axis_index(line), oldest, lax.axis_index(tensor)]
    ).astype(jnp.int32)
    ada = jnp.transpose(ada_weight, (1, 0, 2))
    w = jnp.transpose(qkv_weight, (1, 0, 2))
    mod = modulation(levels, ada)
    mods = lax.all_gather(mod, tensor, axis=0, tiled=False)
    hidden, kv = keys_values(latents, mods, w, k_gain[None])
    kv_all = lax.all_gather(kv, line, axis=0, tiled=False)
    sent = query_parts(scal, hidden, w, q_gain[None], kv, latents, mod)
    came = lax.all_to_all(sent, columns, 0, 0)
    extra = lax.dynamic_slice(
        came, (oldest // LINE, QROWS, 0), (1, EXTRA, HD)
    )[0]
    rows = extra[:128].reshape(8, LINE, 2, HD).transpose(1, 0, 2, 3).reshape(LINE, 16, HD)
    onward = jnp.concatenate(
        [rows, jnp.broadcast_to(extra[128:][None], (LINE, 16, HD))], axis=1
    )
    arrived = lax.all_to_all(onward, line, 0, 0)
    leaving = lax.dynamic_slice(arrived, (oldest % LINE, 0, 0), (1, 32, HD))[0]
    partial = partial_attention(scal, came, kv_all)
    back = lax.all_to_all(partial, columns, 0, 0)
    parts = output_parts(back, leaving, out_weight)
    parts = lax.all_to_all(parts, tensor, 0, 0)
    return finish(scal, parts, latents, mod, leaving, fresh_noise)


def solution(mesh):
    fine = Mesh(mesh.devices.reshape(2, 4, 8, 2, 2), ("yh", "x", "z", "yl", "core"))
    seq, tensor = ("yh", "x", "z"), ("yl", "core")
    return jax.shard_map(
        local,
        mesh=fine,
        in_specs=(
            P(seq, None),
            P(seq),
            P(),
            P(None, tensor),
            P(None, None, tensor),
            P(None, None, tensor),
            P(),
            P(),
            P(tensor, None),
        ),
        out_specs=(P(seq, tensor), P(seq, tensor)),
        check_vma=False,
    )
```

time: 967 us -> 113 us (0.12)
  the two profiles are of different devices: /device:TPU:8 before, /device:TPU:1 now
where the time goes in v1:
time: 113 us; the launch traced here: 112 us
  waiting for transfers between devices  29.7 us (26%)
  blocking collectives  27.5 us (24%)
  starting transfers between devices  19.6 us (17%)
  between operations  15.5 us (14%)
  Pallas kernels  15.1 us (13%)
  local copies, waits for them, and re-layouts  4.21 us (4%)
    all_to_all x1, blocking collectives, local(): parts = lax.all_to_all(parts, tensor, 0, 0)  19.1 us
    all_to_all x1, waiting for transfers between devices, local(): came = lax.all_to_all(sent, columns, 0, 0)  17.7 us
    all_to_all x1, waiting for transfers between devices, local(): back = lax.all_to_all(partial, columns, 0, 0)  10.7 us
    all_gather x1, blocking collectives, local(): mods = lax.all_gather(mod, tensor, axis=0, tiled=False)  8.37 us
    all_to_all x1, starting transfers between devices, local(): arrived = lax.all_to_all(onward, line, 0, 0)  8.18 us
    all_to_all x1, starting transfers between devices, local(): back = lax.all_to_all(partial, columns, 0, 0)  6.48 us
    pallas_call x1, Pallas kernels, partial_attention(): pl.pallas_call(attention_kernel, out_shape=jax.ShapeDtypeStruct((COLS, BA...  5.15 us
    all_to_all x1, starting transfers between devices, local(): came = lax.all_to_all(sent, columns, 0, 0)  4.91 us
  transfers between devices with their start and end apart: 4, of which 3 were waited for; matrix products, arithmetic and copies ran while one was open for 1% of the time, Pallas kernels for 8%

profile of v1, /device:TPU:1, one launch (start us, length us, event | category | flops | bytes accessed | tf_op | source)
XLA Modules:
  0.0 112.3 jit_solution(515495892434432342)
XLA Ops:
  7.2 0.0 copy-start
  7.2 0.0 all-gather.4.cloned.1.call-start
  7.9 0.0 copy-start.3
  7.9 1.2 %copy-done.3 = bf16[256,3,640]{2,0,1:T(8,128)(2,1)S(1)} copy-done((bf16[256,3,640]{2,0,1:T(8,128)(2,1)S(1)}, bf16[256,3,640]{2,0,1:T(8,128)(2,1)}, u32[]{:S(2)}) %copy-start.3) | copy-done | bytes 983064
  9.1 0.0 copy-start.6
  9.1 0.3 modulation.1.mod_ref
  9.4 8.4 %all-gather = f32[32,640]{1,0:T(8,128)S(1)} all-gather(f32[8,640]{1,0:T(8,128)S(1)} %modulation.1.mod_ref), channel_id=2, replica_groups=mesh['yh'=2,'x'=4,'z'=8,'yl'=2,'core'=2] {'yl','core'}, dimensions={0}, use_global_device_ids=true | all-gather | bytes 102400 | tf_op jit(solution)/shard_map/all_gather | solution.py:302
  17.8 0.0 copy-done
  17.8 0.0 copy-done.6
  17.8 0.0 copy-start.5
  17.8 3.9 %keys_values.1 = (bf16[128,2560]{1,0:T(8,128)(2,1)S(1)}, bf16[768,128]{1,0:T(8,128)(2,1)}) custom-call(bf16[128,2560]{1,0:T(8,128)(2,1)S(1)} %copy-done, f32[4,8,640]{2,1,0:T(8,128)S(1)} %bitcast.24, bf16[3,2560,384]{2,1,0:T(8,128)(2,1)} %bitcast.27, f32[1,128]{1,0:T(1,128)S(1)} %bitcast.26), custom_call_target="tpu_custom_call" | custom-call | tf_op jit(solution)/shard_map/keys_values/pallas_call | solution.py:113
  21.7 0.0 all-gather.4.cloned.1.call-update
  22.4 0.1 pad_add_fusion.scal_ref
  22.4 0.0 copy-done.5
  22.4 3.6 %queries.1 = bf16[8,528,128]{2,1,0:T(8,128)(2,1)} custom-call(s32[4]{0:T(128)S(1)} %pad_add_fusion.scal_ref, bf16[128,2560]{1,0:T(8,128)(2,1)S(1)} %get-tuple-element.4.hidden_ref, bf16[3,2560,384]{2,1,0:T(8,128)(2,1)} %bitcast.28, f32[1,128]{1,0:T(1,128)S(1)} %bitcast.25, bf16[768,128]{1,0:T(8,128)(2,1)} %get-tuple-element.5.kv_ref, ...), custom_call_target="tpu_custom_call" | custom-call | tf_op jit(solution)/shard_map/queries/pallas_call | solution.py:164
  26.0 4.9 %all-to-all-start = ((bf16[8,528,128]{2,1,0:T(8,128)(2,1)}), bf16[8,528,128]{2,1,0:T(8,128)(2,1)S(1)}, u32[]{:S(2)}, u32[]{:S(2)}) async-start(bf16[8,528,128]{2,1,0:T(8,128)(2,1)} %queries.1), calls=%async_computation | async-start | bytes 2162688 | tf_op jit(solution)/shard_map/all_to_all | solution.py:306
  30.9 17.7 %all-to-all-done.q_ref = bf16[8,528,128]{2,1,0:T(8,128)(2,1)S(1)} async-done(((bf16[8,528,128]{2,1,0:T(8,128)(2,1)}), bf16[8,528,128]{2,1,0:T(8,128)(2,1)S(1)}, u32[]{:S(2)}, u32[]{:S(2)}) %all-to-all-start) | async-done | bytes 1081376 | tf_op jit(solution)/shard_map/all_to_all | solution.py:306
  48.7 0.6 pad_maximum_fusion
  49.4 8.2 %all-to-all-start.2 = ((bf16[8,32,128]{2,1,0:T(8,128)(2,1)}), bf16[8,32,128]{2,1,0:T(8,128)(2,1)S(1)}, u32[]{:S(2)}, u32[]{:S(2)}) async-start(bf16[8,32,128]{2,1,0:T(8,128)(2,1)} %pad_maximum_fusion), calls=%async_computation.2 | async-start | bytes 131072 | tf_op jit(solution)/shard_map/all_to_all | solution.py:314
  57.5 1.2 %all-gather.4.cloned.1.call-done = bf16[6144,128]{1,0:T(8,128)(2,1)} async-done(((bf16[768,128]{1,0:T(8,128)(2,1)}), bf16[6144,128]{1,0:T(8,128)(2,1)}) %all-gather.4.cloned.1.call-update) | async-done | bytes 1572880 | tf_op jit(solution)/shard_map/all_gather | solution.py:304
  58.8 0.0 copy-start.2
  58.8 1.4 %copy-done.2 = bf16[6144,128]{1,0:T(8,128)(2,1)S(1)} copy-done((bf16[6144,128]{1,0:T(8,128)(2,1)S(1)}, bf16[6144,128]{1,0:T(8,128)(2,1)}, u32[]{:S(2)}) %copy-start.2) | copy-done | bytes 1572888
  60.2 5.1 %attention.1 = bf16[8,400,128]{2,1,0:T(8,128)(2,1)} custom-call(s32[4]{0:T(128)S(1)} %pad_add_fusion.scal_ref, bf16[8,528,128]{2,1,0:T(8,128)(2,1)S(1)} %all-to-all-done.q_ref, bf16[8,768,128]{2,1,0:T(8,128)(2,1)S(1)} %bitcast.22), custom_call_target="tpu_custom_call" | custom-call | tf_op jit(solution)/shard_map/attention/pallas_call | solution.py:221
  65.4 0.0 all-to-all-done.2
  65.4 6.5 %all-to-all-start.1 = ((bf16[8,400,128]{2,1,0:T(8,128)(2,1)}), bf16[8,400,128]{2,1,0:T(8,128)(2,1)S(1)}, u32[]{:S(2)}, u32[]{:S(2)}) async-start(bf16[8,400,128]{2,1,0:T(8,128)(2,1)} %attention.1), calls=%async_computation.1 | async-start | bytes 1638400 | tf_op jit(solution)/shard_map/all_to_all | solution.py:317
  71.8 10.7 %all-to-all-done.1.back_ref = bf16[8,400,128]{2,1,0:T(8,128)(2,1)S(1)} async-done(((bf16[8,400,128]{2,1,0:T(8,128)(2,1)}), bf16[8,400,128]{2,1,0:T(8,128)(2,1)S(1)}, u32[]{:S(2)}, u32[]{:S(2)}) %all-to-all-start.1) | async-done | bytes 819232 | tf_op jit(solution)/shard_map/all_to_all | solution.py:317
  82.5 1.5 %copy-done.1 = bf16[384,2560]{1,0:T(8,128)(2,1)S(1)} copy-done((bf16[384,2560]{1,0:T(8,128)(2,1)S(1)}, bf16[384,2560]{1,0:T(8,128)(2,1)}, u32[]{:S(2)}) %copy-start.1) | copy-done | bytes 1966104
  84.1 0.9 output.1
  85.0 0.0 copy-start.4
  85.0 19.1 %all_to_all.20.parts_ref = bf16[4,144,640]{2,1,0:T(8,128)(2,1)S(1)} all-to-all(bf16[4,144,640]{2,1,0:T(8,128)(2,1)S(1)} %output.1), channel_id=1, replica_groups=mesh['yh'=2,'x'=4,'z'=8,'yl'=2,'core'=2] {'yl','core'}, dimensions={0} | all-to-all | bytes 1474560 | tf_op jit(solution)/shard_map/all_to_all | solution.py:319
  104.1 0.0 copy-done.4
  104.1 1.4 %finish.1 = (bf16[128,640]{1,0:T(8,128)(2,1)}, bf16[2,640]{1,0:T(2,128)(2,1)}) custom-call(s32[4]{0:T(128)S(1)} %pad_add_fusion.scal_ref, bf16[4,144,640]{2,1,0:T(8,128)(2,1)S(1)} %all_to_all.20.parts_ref, bf16[128,2560]{1,0:T(8,128)(2,1)S(1)} %copy-done, f32[8,640]{1,0:T(8,128)S(1)} %modulation.1.mod_ref, ...), custom_call_target="tpu_custom_call" | custom-call | tf_op jit(solution)/shard_map/finish/pallas_call | solution.py:278
  (6 shorter events, 0.1 us)
Async XLA Ops:
  7.2 10.6 %copy-start = (bf16[128,2560]{1,0:T(8,128)(2,1)S(1)}, bf16[128,2560]{1,0:T(8,128)(2,1)}, u32[]{:S(2)}) copy-start(bf16[128,2560]{1,0:T(8,128)(2,1)} %lat_ref.5) | copy-start | bytes 1966084
  7.2 51.6 %all-gather.4.cloned.1.call-start = ((), (), s32[]{:S(2)}) async-start(), calls=%async_computation.4 | async-start | bytes 1769472 | tf_op jit(solution)/shard_map/all_gather | solution.py:304
  7.9 1.2 %copy-start.3 = (bf16[256,3,640]{2,0,1:T(8,128)(2,1)S(1)}, bf16[256,3,640]{2,0,1:T(8,128)(2,1)}, u32[]{:S(2)}) copy-start(bf16[256,3,640]{2,0,1:T(8,128)(2,1)} %param.13) | copy-start | bytes 2949124
  9.1 8.6 %copy-start.6 = (f32[128]{0:T(128)S(1)}, f32[128]{0:T(128)}, u32[]{:S(2)}) copy-start(f32[128]{0:T(128)} %param.16) | copy-start | bytes 1540
  17.8 4.7 %copy-start.5 = (f32[128]{0:T(128)S(1)}, f32[128]{0:T(128)}, u32[]{:S(2)}) copy-start(f32[128]{0:T(128)} %param.15) | copy-start | bytes 1540
  26.0 22.7 %all-to-all-start = ((bf16[8,528,128]{2,1,0:T(8,128)(2,1)}), bf16[8,528,128]{2,1,0:T(8,128)(2,1)S(1)}, u32[]{:S(2)}, u32[]{:S(2)}) async-start(bf16[8,528,128]{2,1,0:T(8,128)(2,1)} %queries.1), calls=%async_computation | async-start | bytes 2162688 | tf_op jit(solution)/shard_map/all_to_all | solution.py:306
  49.4 16.0 %all-to-all-start.2 = ((bf16[8,32,128]{2,1,0:T(8,128)(2,1)}), bf16[8,32,128]{2,1,0:T(8,128)(2,1)S(1)}, u32[]{:S(2)}, u32[]{:S(2)}) async-start(bf16[8,32,128]{2,1,0:T(8,128)(2,1)} %pad_maximum_fusion), calls=%async_computation.2 | async-start | bytes 131072 | tf_op jit(solution)/shard_map/all_to_all | solution.py:314
  58.8 1.4 %copy-start.2 = (bf16[6144,128]{1,0:T(8,128)(2,1)S(1)}, bf16[6144,128]{1,0:T(8,128)(2,1)}, u32[]{:S(2)}) copy-start(bf16[6144,128]{1,0:T(8,128)(2,1)} %all-gather.4.cloned.1.call-done) | copy-start | bytes 4718596
  65.4 17.2 %all-to-all-start.1 = ((bf16[8,400,128]{2,1,0:T(8,128)(2,1)}), bf16[8,400,128]{2,1,0:T(8,128)(2,1)S(1)}, u32[]{:S(2)}, u32[]{:S(2)}) async-start(bf16[8,400,128]{2,1,0:T(8,128)(2,1)} %attention.1), calls=%async_computation.1 | async-start | bytes 1638400 | tf_op jit(solution)/shard_map/all_to_all | solution.py:317
  82.5 1.5 %copy-start.1 = (bf16[384,2560]{1,0:T(8,128)(2,1)S(1)}, bf16[384,2560]{1,0:T(8,128)(2,1)}, u32[]{:S(2)}) copy-start(bf16[384,2560]{1,0:T(8,128)(2,1)} %w_ref.1) | copy-start | bytes 5898244
  85.0 19.2 %copy-start.4 = (bf16[128,640]{1,0:T(8,128)(2,1)S(1)}, bf16[128,640]{1,0:T(8,128)(2,1)}, u32[]{:S(2)}) copy-start(bf16[128,640]{1,0:T(8,128)(2,1)} %fresh_ref.1) | copy-start | bytes 491524
Sparse Core Ops, SparseCore 0:
  21.8 36.9 all-gather.3

commit v2 on v0

v2 whole, which is shorter than its diff:
```python
import functools
import math

import jax
import jax.numpy as jnp
from jax import lax
from jax.experimental import pallas as pl
from jax.experimental.pallas import tpu as pltpu
from jax.sharding import Mesh
from jax.sharding import PartitionSpec as P

F32 = jnp.float32
BF16 = jnp.bfloat16
COLS = 8
LINE = 8
BLOCKS = COLS * LINE
ROWS = 128
HD = 128
NH = 3
D = 2560
QW = D // 4
QROWS = NH * ROWS
KV = 2 * QROWS
EXTRA = 144
SEND = KV + EXTRA
BACK = QROWS + 16
RETURN = BACK + 32
OUTROWS = ROWS + 16
AWAY = (0, -1, 1, -2, 2, -3, 3, 4)
TURNS = ((6, 7), (4, 5), (2, 3), (0, 1))


def vmem(n):
    return [pl.BlockSpec(memory_space=pltpu.VMEM)] * n


def hbm():
    return pl.BlockSpec(memory_space=pltpu.MemorySpace.HBM)


def smem():
    return pl.BlockSpec(memory_space=pltpu.SMEM)


def params(mib=48):
    return pltpu.CompilerParams(vmem_limit_bytes=mib << 20)


def dot(a, b):
    return jnp.dot(a, b, preferred_element_type=F32)


def dot_t(a, b):
    return lax.dot_general(a, b, (((1,), (1,)), ((), ())), preferred_element_type=F32)


def opening_kernel(
    level_ref, scal_ref, ada_ref, lat_ref, qg_ref, kg_ref, mod_ref, normed_ref, own_ref
):
    half = 128
    index = lax.broadcasted_iota(jnp.int32, (16, 2 * half), 1)
    place = jnp.where(index < half, index, index - half).astype(F32)
    frequency = jnp.exp(-math.log(10000.0) * place / half)
    angle = level_ref[0].astype(F32) * frequency
    wave = jnp.where(index < half, jnp.cos(angle), jnp.sin(angle))
    embedding = (wave * (1.0 / (1.0 + jnp.exp(-wave)))).astype(BF16)
    for j in range(3):
        mod_ref[pl.ds(j, 1), :] = dot(embedding, ada_ref[j])[0:1]
    mod_ref[3:4, 0:HD] = qg_ref[...]
    mod_ref[4:5, 0:HD] = kg_ref[...]
    states = lat_ref[...].astype(F32)
    average = jnp.mean(states, axis=-1, keepdims=True)
    centered = states - average
    variance = jnp.mean(centered * centered, axis=-1, keepdims=True)
    normed_ref[...] = centered * lax.rsqrt(variance + 1e-06)
    first = pl.multiple_of(scal_ref[3] * QW, 128)
    for k in range(5):
        own_ref[:, k * 128 : (k + 1) * 128] = lat_ref[:, pl.ds(first + k * 128, 128)]


def opening(levels, scal, ada, latents, q_gain, k_gain):
    return pl.pallas_call(
        opening_kernel,
        out_shape=(
            jax.ShapeDtypeStruct((8, QW), F32),
            jax.ShapeDtypeStruct((ROWS, D), F32),
            jax.ShapeDtypeStruct((ROWS, QW), BF16),
        ),
        in_specs=[smem(), smem()] + vmem(4),
        out_specs=tuple(vmem(3)),
        compiler_params=params(16),
        name="opening",
    )(levels, scal, ada, latents, q_gain, k_gain)


def rms_rounded(matrix, gain, factor):
    power = jnp.mean(matrix * matrix, axis=-1, keepdims=True)
    return (matrix * lax.rsqrt(power + 1e-06) * gain * factor).astype(BF16)


def front_kernel(
    normed_ref, mods_ref, mod_ref, own_ref, w_ref, q_ref, out_ref, hidden_ref, piece_ref, cut_ref
):
    for t in range(4):
        piece = normed_ref[:, t * QW : (t + 1) * QW]
        shift = mods_ref[t, 0:1, :]
        scale = mods_ref[t, 1:2, :]
        hidden_ref[:, t * QW : (t + 1) * QW] = (piece * (1.0 + scale) + shift).astype(BF16)
    for k in range(5):
        piece_ref[NH + k] = own_ref[:, k * 128 : (k + 1) * 128].astype(F32)
    rows = [mod_ref[2:3, k * 128 : (k + 1) * 128] for k in range(5)]
    high = [row.astype(BF16).astype(F32) for row in rows]
    low = [row - top for row, top in zip(rows, high)]
    gate = jnp.concatenate(high + low + [jnp.zeros((6, 128), F32)], axis=0).astype(BF16)
    hidden = hidden_ref[...]
    keys_all = dot(hidden, w_ref[1])
    values_all = dot(hidden, w_ref[2])
    queries_all = dot(hidden, w_ref[0])
    for h in range(NH):
        at = slice(h * HD, (h + 1) * HD)
        keys = rms_rounded(keys_all[:, at], mod_ref[4:5, 0:HD], 1.0)
        values = values_all[:, at].astype(BF16)
        q = rms_rounded(queries_all[:, at], mod_ref[3:4, 0:HD], 1.0 / math.sqrt(HD))
        q_ref[at, :] = q
        for c in range(COLS):
            out_ref[c, h * ROWS : (h + 1) * ROWS, :] = keys
            out_ref[c, QROWS + h * ROWS : QROWS + (h + 1) * ROWS, :] = values
        weights = jnp.exp(dot_t(q, keys))
        total = jnp.sum(weights, axis=-1, keepdims=True)
        attended = (dot(weights.astype(BF16), values) / total).astype(BF16)
        piece_ref[h] = attended.astype(F32)
    for k in range(8):
        for r in range(2):
            cut_ref[pl.ds(2 * k + r, BLOCKS, stride=16), :] = piece_ref[
                k, pl.ds(r, BLOCKS, stride=2), :
            ]
    for c in range(COLS):
        out_ref[c, KV : KV + 128, :] = cut_ref[c * 128 : (c + 1) * 128, :].astype(BF16)
        out_ref[c, KV + 128 : SEND, :] = gate


def front(normed, mods, mod, own, w):
    return pl.pallas_call(
        front_kernel,
        out_shape=(
            jax.ShapeDtypeStruct((QROWS, HD), BF16),
            jax.ShapeDtypeStruct((COLS, SEND, HD), BF16),
        ),
        in_specs=vmem(5),
        out_specs=tuple(vmem(2)),
        scratch_shapes=[
            pltpu.VMEM((ROWS, D), BF16),
            pltpu.VMEM((8, ROWS, 128), F32),
            pltpu.VMEM((BLOCKS * 16, 128), F32),
        ],
        compiler_params=params(16),
        name="front",
    )(normed, mods, mod, own, w)


def attention_kernel(slots, scal_ref, qa_ref, qb_ref, came_ref, *out_refs):
    column, line, oldest = scal_ref[0], scal_ref[1], scal_ref[2]
    key_block = lax.broadcasted_iota(jnp.int32, (1, COLS * ROWS), 1) // ROWS
    key_rank = (key_block * LINE + line - oldest) & (BLOCKS - 1)
    ranks, places = [], []
    for slot in slots:
        places.append((line + AWAY[slot]) & (LINE - 1))
        ranks.append((column * LINE + places[-1] - oldest) & (BLOCKS - 1))
    upper = lax.broadcasted_iota(jnp.int32, (2 * ROWS, 1), 0) < ROWS
    seen = key_rank <= jnp.where(upper, ranks[0], ranks[1])
    lane = lax.broadcasted_iota(jnp.int32, (ROWS, 128), 1)
    totals = []
    for h in range(NH):
        at = slice(h * ROWS, (h + 1) * ROWS)
        q = jnp.concatenate([qa_ref[at, :], qb_ref[at, :]], axis=0)
        keys = came_ref[:, at, :].reshape(COLS * ROWS, HD)
        values = came_ref[:, QROWS + h * ROWS : QROWS + (h + 1) * ROWS, :].reshape(
            COLS * ROWS, HD
        )
        weights = jnp.where(seen, jnp.exp(dot_t(q, keys)), 0.0)
        totals.append(jnp.sum(weights, axis=-1, keepdims=True))
        products = dot(weights.astype(BF16), values)
        for b in range(2):
            out_refs[b][at, :] = products[b * ROWS : (b + 1) * ROWS].astype(out_refs[b].dtype)
    root = oldest // LINE
    mine = line == (oldest & (LINE - 1))
    for b in range(2):
        tile = jnp.zeros((ROWS, 128), F32)
        for h in range(NH):
            total = totals[h][b * ROWS : (b + 1) * ROWS]
            tile = jnp.where(lane == h, total, tile)
        out_refs[b][QROWS:BACK, :] = parted(tile.T[0:8]).astype(out_refs[b].dtype)
        at = pl.multiple_of(KV + places[b] * 16, 16)
        extra = jnp.concatenate(
            [came_ref[root, pl.ds(at, 16), :], came_ref[root, KV + 128 : SEND, :]], axis=0
        ).astype(F32)
        out_refs[b][BACK:RETURN, :] = jnp.where(mine, extra, 0.0).astype(out_refs[b].dtype)


def parted(totals):
    high = totals.astype(BF16).astype(F32)
    return jnp.concatenate([high, totals - high], axis=0)


def partial_attention(scal, slots, queries, came, kind):
    shape = jax.ShapeDtypeStruct((RETURN, HD), kind)
    return pl.pallas_call(
        functools.partial(attention_kernel, slots),
        out_shape=(shape, shape),
        in_specs=[smem()] + vmem(3),
        out_specs=tuple(vmem(2)),
        compiler_params=params(16),
        name="attention",
    )(scal, *[queries[slot] for slot in slots], came)


def joined_kernel(*refs):
    count = len(refs) // 3
    for i in range(count):
        came_ref, own_ref, out_ref = refs[i], refs[count + i], refs[2 * count + i]
        sums = came_ref[...].astype(F32) + own_ref[...]
        out_ref[0:QROWS, :] = sums[0:QROWS].astype(BF16)
        out_ref[QROWS:BACK, :] = parted(sums[QROWS : QROWS + 8] + sums[QROWS + 8 : BACK]).astype(
            BF16
        )
        out_ref[BACK:RETURN, :] = sums[BACK:RETURN].astype(BF16)


def joined(came, own):
    shape = jax.ShapeDtypeStruct((RETURN, HD), BF16)
    return pl.pallas_call(
        joined_kernel,
        out_shape=(shape,) * len(came),
        in_specs=vmem(2 * len(came)),
        out_specs=tuple(vmem(len(came))),
        compiler_params=params(16),
        name="joined",
    )(*came, *own)


def combine_kernel(up_ref, down_ref, own_ref, out_ref, leaving_ref):
    sums = up_ref[...].astype(F32) + down_ref[...].astype(F32) + own_ref[...]
    leaving = sums[BACK:RETURN]
    leaving_ref[...] = leaving
    totals = sums[QROWS : QROWS + 8] + sums[QROWS + 8 : BACK]
    tile = jnp.concatenate([totals, jnp.zeros((ROWS - 8, 128), F32)], axis=0).T
    for h in range(NH):
        total = tile[:, h : h + 1]
        out_ref[0:ROWS, h * HD : (h + 1) * HD] = (sums[h * ROWS : (h + 1) * ROWS] / total).astype(
            BF16
        )
        out_ref[ROWS:OUTROWS, h * HD : (h + 1) * HD] = jnp.concatenate(
            [leaving[2 * h : 2 * h + 2], jnp.zeros((14, HD), F32)], axis=0
        ).astype(BF16)


def combine(up, down, own):
    return pl.pallas_call(
        combine_kernel,
        out_shape=(
            jax.ShapeDtypeStruct((OUTROWS, QROWS), BF16),
            jax.ShapeDtypeStruct((32, HD), F32),
        ),
        in_specs=vmem(3),
        out_specs=tuple(vmem(2)),
        compiler_params=params(16),
        name="combine",
    )(up, down, own)


def finish_kernel(
    scal_ref, att_ref, w1_ref, w2_ref, w3_ref, own_ref, mod_ref, leaving_ref, fresh_ref, w_ref,
    window_ref, clean_ref, w_held, sem,
):
    tensor = scal_ref[3]
    first = pl.multiple_of(tensor * QW, 128)
    copy = pltpu.make_async_copy(w_ref.at[:, pl.ds(first, QW)], w_held, sem)
    copy.start()
    projected = dot(att_ref[tensor ^ 1], w1_ref[...])
    projected = projected + dot(att_ref[tensor ^ 2], w2_ref[...])
    projected = projected + dot(att_ref[tensor ^ 3], w3_ref[...])
    copy.wait()
    projected = projected + dot(att_ref[tensor], w_held[...])
    oldest = scal_ref[0] * LINE + scal_ref[1] == scal_ref[2]
    leaving = leaving_ref[...]
    for k in range(5):
        at = slice(k * 128, (k + 1) * 128)
        states = own_ref[:, at].astype(F32)
        updated = (states + mod_ref[2:3, at] * projected[0:ROWS, at]).astype(BF16)
        window_ref[:, at] = jnp.where(oldest, fresh_ref[:, at], updated)
        gate = leaving[16 + k : 17 + k] + leaving[21 + k : 22 + k]
        old = leaving[2 * (NH + k) : 2 * (NH + k) + 2]
        clean_ref[:, at] = (old + gate * projected[ROWS : ROWS + 2, at]).astype(BF16)


def finish(scal, attended, pieces, own, mod, leaving, fresh, w):
    return pl.pallas_call(
        finish_kernel,
        out_shape=(
            jax.ShapeDtypeStruct((ROWS, QW), BF16),
            jax.ShapeDtypeStruct((2, QW), BF16),
        ),
        in_specs=[smem()] + vmem(8) + [hbm()],
        out_specs=tuple(vmem(2)),
        scratch_shapes=[pltpu.VMEM((QROWS, QW), BF16), pltpu.SemaphoreType.DMA],
        compiler_params=params(16),
        name="finish",
    )(scal, attended, *pieces, own, mod, leaving, fresh, w)


COLUMN, TENSOR = ("yh", "x"), ("yl", "core")


def shifted(array, step):
    return lax.ppermute(array, "z", [(i, (i + step) % LINE) for i in range(LINE)])


def ring(own):
    pieces, up, down = [own], own, own
    for step in range(LINE // 2):
        up = shifted(up, 1)
        pieces.append(up)
        if step < LINE // 2 - 1:
            down = shifted(down, -1)
            pieces.append(down)
    return pieces


def exchanged(weight, after):
    place = lax.axis_index(TENSOR)
    weight, _ = lax.optimization_barrier((weight, after))
    return [
        lax.ppermute(
            lax.dynamic_slice_in_dim(weight, (place ^ d) * QW, QW, 1),
            TENSOR,
            [(i, i ^ d) for i in range(4)],
        )
        for d in (1, 2, 3)
    ]


def local(
    latents, levels, head_slot, fresh_noise, ada_weight, qkv_weight, q_gain, k_gain, out_weight
):
    oldest = head_slot[0]
    scal = jnp.stack(
        [lax.axis_index(COLUMN), lax.axis_index("z"), oldest, lax.axis_index(TENSOR)]
    ).astype(jnp.int32)
    ada = jnp.transpose(ada_weight, (1, 0, 2))
    w = jnp.transpose(qkv_weight, (1, 0, 2))
    mod, normed, own = opening(levels, scal, ada, latents, q_gain[None], k_gain[None])
    mods = lax.all_gather(mod, TENSOR, axis=0, tiled=False)
    q, sent = front(normed, mods, mod, own, w)
    came = lax.all_to_all(sent, COLUMN, 0, 0)
    queries = ring(q)
    came, *queries = lax.optimization_barrier((came, *queries))
    up, down = partial_attention(scal, TURNS[0], queries, came, BF16)
    weights = exchanged(out_weight, down)
    for turn in (1, 2):
        up, down = shifted(up, 1), shifted(down, -1)
        up, down = joined(
            (up, down), partial_attention(scal, TURNS[turn], queries, came, F32)
        )
    up, down = shifted(up, 1), shifted(down, -1)
    still, last = partial_attention(scal, TURNS[3], queries, came, F32)
    still, weights = lax.optimization_barrier((still, weights))
    down = shifted(joined((down,), (last,))[0], -1)
    attended, leaving = combine(up, down, still)
    attended = lax.all_gather(attended, TENSOR, axis=0, tiled=False)
    return finish(scal, attended, weights, own, mod, leaving, fresh_noise, out_weight)


def solution(mesh):
    fine = Mesh(mesh.devices.reshape(2, 4, 8, 2, 2), ("yh", "x", "z", "yl", "core"))
    seq, tensor = ("yh", "x", "z"), ("yl", "core")
    return jax.shard_map(
        local,
        mesh=fine,
        in_specs=(
            P(seq, None),
            P(seq),
            P(),
            P(None, tensor),
            P(None, None, tensor),
            P(None, None, tensor),
            P(),
            P(),
            P(tensor, None),
        ),
        out_specs=(P(seq, tensor), P(seq, tensor)),
        check_vma=False,
    )
```

time: 967 us -> 92.5 us (0.10)
  the two profiles are of different devices: /device:TPU:8 before, /device:TPU:1 now
where the time goes in v2:
time: 92.5 us; the launch traced here: 92.1 us
  starting transfers between devices  32.8 us (35%)
  waiting for transfers between devices  19.3 us (21%)
  blocking collectives  18.6 us (20%)
  Pallas kernels  11.5 us (12%)
  local copies, waits for them, and re-layouts  7.66 us (8%)
  between operations  2.2 us (2%)
    ppermute x14, starting transfers between devices, shifted(): lax.ppermute(array, 'z', [(i, (i + step) % LINE) for i in range(LINE)])  25.3 us
    ppermute x14, waiting for transfers between devices, shifted(): lax.ppermute(array, 'z', [(i, (i + step) % LINE) for i in range(LINE)])  16.2 us
    all_gather x1, blocking collectives, local(): attended = lax.all_gather(attended, TENSOR, axis=0, tiled=False)  10.3 us
    all_gather x1, blocking collectives, local(): mods = lax.all_gather(mod, TENSOR, axis=0, tiled=False)  8.36 us
    unnamed x16, local copies, waits for them, and re-layouts  7.52 us
    pallas_call x4, Pallas kernels, partial_attention(): pl.pallas_call(functools.partial(attention_kernel, slots), out_shape=(sha...  6.26 us
    all_to_all x1, starting transfers between devices, local(): came = lax.all_to_all(sent, COLUMN, 0, 0)  4.91 us
    all_to_all x1, waiting for transfers between devices, local(): came = lax.all_to_all(sent, COLUMN, 0, 0)  2.89 us
  transfers between devices with their start and end apart: 18, of which 11 were waited for; matrix products, arithmetic and copies ran while one was open for 0% of the time, Pallas kernels for 5%

profile of v2, /device:TPU:1, one launch (start us, length us, event | category | flops | bytes accessed | tf_op | source)
XLA Modules:
  0.0 92.1 jit_solution(1046126350863659433)
XLA Ops:
  2.0 1.2 %copy-done.3 = bf16[256,3,640]{2,0,1:T(8,128)(2,1)S(1)} copy-done((bf16[256,3,640]{2,0,1:T(8,128)(2,1)S(1)}, bf16[256,3,640]{2,0,1:T(8,128)(2,1)}, u32[]{:S(2)}) %copy-start.3) | copy-done | bytes 983064
  3.2 1.1 %copy-done.4 = bf16[128,2560]{1,0:T(8,128)(2,1)S(1)} copy-done((bf16[128,2560]{1,0:T(8,128)(2,1)S(1)}, bf16[128,2560]{1,0:T(8,128)(2,1)}, u32[]{:S(2)}) %copy-start.4) | copy-done | bytes 655384
  5.6 1.0 %opening.1 = (f32[8,640]{1,0:T(8,128)S(1)}, f32[128,2560]{1,0:T(8,128)S(1)}, bf16[128,640]{1,0:T(8,128)(2,1)S(1)}) custom-call(s32[1]{0:T(128)S(6)} %copy.11.level_ref, s32[4]{0:T(128)S(1)} %pad_add_fusion.scal_ref, bf16[3,256,640]{2,1,0:T(8,128)(2,1)S(1)} %bitcast.11, bf16[128,2560]{1,0:T(8,128)(2,1)S(1)} %copy-done.4, f32[1,128]{1,0:T(1,128)S(1)} %bitcast.13, ...), custom_call_target="tpu_custom_call" | custom-call | tf_op jit(solution)/shard_map/opening/pallas_call | solution.py:82
  6.6 8.4 %all-gather = f32[32,640]{1,0:T(8,128)S(1)} all-gather(f32[8,640]{1,0:T(8,128)S(1)} %get-tuple-element.36.mod_ref), channel_id=2, replica_groups=mesh['yh'=2,'x'=4,'z'=8,'yl'=2,'core'=2] {'yl','core'}, dimensions={0}, use_global_device_ids=true | all-gather | bytes 102400 | tf_op jit(solution)/shard_map/all_gather | solution.py:352
  15.0 2.7 %copy-done.1 = bf16[2560,3,384]{2,0,1:T(8,128)(2,1)S(1)} copy-done((bf16[2560,3,384]{2,0,1:T(8,128)(2,1)S(1)}, bf16[2560,3,384]{2,0,1:T(8,128)(2,1)}, u32[]{:S(2)}) %copy-start.1) | copy-done | bytes 5898264
  17.6 1.8 %front.1 = (bf16[384,128]{1,0:T(8,128)(2,1)S(1)}, bf16[8,912,128]{2,1,0:T(8,128)(2,1)S(1)}) custom-call(f32[128,2560]{1,0:T(8,128)S(1)} %get-tuple-element.35.normed_ref, f32[4,8,640]{2,1,0:T(8,128)S(1)} %bitcast.12, f32[8,640]{1,0:T(8,128)S(1)} %get-tuple-element.36.mod_ref, bf16[128,640]{1,0:T(8,128)(2,1)S(1)} %get-tuple-element.37.own_ref, ...), custom_call_target="tpu_custom_call" | custom-call | tf_op jit(solution)/shard_map/front/pallas_call | solution.py:143
  19.4 1.2 %copy-done.2 = bf16[8,912,128]{2,1,0:T(8,128)(2,1)} copy-done((bf16[8,912,128]{2,1,0:T(8,128)(2,1)}, bf16[8,912,128]{2,1,0:T(8,128)(2,1)S(1)}, u32[]{:S(2)}) %copy-start.2) | copy-done | bytes 1867800
  20.7 4.9 %all-to-all-start = ((bf16[8,912,128]{2,1,0:T(8,128)(2,1)}), bf16[8,912,128]{2,1,0:T(8,128)(2,1)S(1)}, u32[]{:S(2)}, u32[]{:S(2)}) async-start(bf16[8,912,128]{2,1,0:T(8,128)(2,1)} %copy-done.2), calls=%async_computation | async-start | bytes 3735552 | tf_op jit(solution)/shard_map/all_to_all | solution.py:354
  25.6 1.6 %collective-permute-start = (bf16[384,128]{1,0:T(8,128)(2,1)S(1)}, bf16[384,128]{1,0:T(8,128)(2,1)S(1)}, u32[]{:S(2)}, u32[]{:S(2)}) collective-permute-start(bf16[384,128]{1,0:T(8,128)(2,1)S(1)} %get-tuple-element.57.qa_ref), channel_id=1, source_target_pairs={{0,4},{4,8},{8,12},{12,16},{16,20},{20,24},{24,28},{28,0},{1,5},{5... | collective-permute-start | bytes 294920 | tf_op jit(solution)/shard_map/ppermute | solution.py:315
  27.2 4.0 %collective-permute-start.1 = (bf16[384,128]{1,0:T(8,128)(2,1)S(1)}, bf16[384,128]{1,0:T(8,128)(2,1)S(1)}, u32[]{:S(2)}, u32[]{:S(2)}) collective-permute-start(bf16[384,128]{1,0:T(8,128)(2,1)S(1)} %get-tuple-element.57.qa_ref), channel_id=1, source_target_pairs={{0,28},{4,0},{8,4},{12,8},{16,12},{20,16},{24,20},{28,24},{1,29},{... | collective-permute-start | bytes 294920 | tf_op jit(solution)/shard_map/ppermute | solution.py:315
  31.2 2.7 %collective-permute-done.qb_ref = bf16[384,128]{1,0:T(8,128)(2,1)S(1)} collective-permute-done((bf16[384,128]{1,0:T(8,128)(2,1)S(1)}, bf16[384,128]{1,0:T(8,128)(2,1)S(1)}, u32[]{:S(2)}, u32[]{:S(2)}) %collective-permute-start) | collective-permute-done | bytes 98336 | tf_op jit(solution)/shard_map/ppermute | solution.py:315
  33.9 2.7 %collective-permute-start.3 = (bf16[384,128]{1,0:T(8,128)(2,1)S(1)}, bf16[384,128]{1,0:T(8,128)(2,1)S(1)}, u32[]{:S(2)}, u32[]{:S(2)}) collective-permute-start(bf16[384,128]{1,0:T(8,128)(2,1)S(1)} %collective-permute-done.1.qa_ref), channel_id=1, source_target_pairs={{0,28},{4,0},{8,4},{12,8},{16,12},{20,16},{24,20},{28,24},{1,29},{... | collective-permute-start | bytes 294920 | tf_op jit(solution)/shard_map/ppermute | solution.py:315
  36.6 2.3 %collective-permute-done.2.qb_ref = bf16[384,128]{1,0:T(8,128)(2,1)S(1)} collective-permute-done((bf16[384,128]{1,0:T(8,128)(2,1)S(1)}, bf16[384,128]{1,0:T(8,128)(2,1)S(1)}, u32[]{:S(2)}, u32[]{:S(2)}) %collective-permute-start.2) | collective-permute-done | bytes 98336 | tf_op jit(solution)/shard_map/ppermute | solution.py:315
  38.9 2.7 %collective-permute-start.5 = (bf16[384,128]{1,0:T(8,128)(2,1)S(1)}, bf16[384,128]{1,0:T(8,128)(2,1)S(1)}, u32[]{:S(2)}, u32[]{:S(2)}) collective-permute-start(bf16[384,128]{1,0:T(8,128)(2,1)S(1)} %collective-permute-done.3.qa_ref), channel_id=1, source_target_pairs={{0,28},{4,0},{8,4},{12,8},{16,12},{20,16},{24,20},{28,24},{1,29},{... | collective-permute-start | bytes 294920 | tf_op jit(solution)/shard_map/ppermute | solution.py:315
  41.6 2.3 %collective-permute-done.4.qb_ref = bf16[384,128]{1,0:T(8,128)(2,1)S(1)} collective-permute-done((bf16[384,128]{1,0:T(8,128)(2,1)S(1)}, bf16[384,128]{1,0:T(8,128)(2,1)S(1)}, u32[]{:S(2)}, u32[]{:S(2)}) %collective-permute-start.4) | collective-permute-done | bytes 98336 | tf_op jit(solution)/shard_map/ppermute | solution.py:315
  43.9 5.0 %collective-permute-done.6.qb_ref = bf16[384,128]{1,0:T(8,128)(2,1)S(1)} collective-permute-done((bf16[384,128]{1,0:T(8,128)(2,1)S(1)}, bf16[384,128]{1,0:T(8,128)(2,1)S(1)}, u32[]{:S(2)}, u32[]{:S(2)}) %collective-permute-start.6) | collective-permute-done | bytes 98336 | tf_op jit(solution)/shard_map/ppermute | solution.py:315
  48.9 2.9 %all-to-all-done.came_ref = bf16[8,912,128]{2,1,0:T(8,128)(2,1)S(1)} async-done(((bf16[8,912,128]{2,1,0:T(8,128)(2,1)}), bf16[8,912,128]{2,1,0:T(8,128)(2,1)S(1)}, u32[]{:S(2)}, u32[]{:S(2)}) %all-to-all-start) | async-done | bytes 1867808 | tf_op jit(solution)/shard_map/all_to_all | solution.py:354
  51.8 1.6 %attention.4 = (bf16[432,128]{1,0:T(8,128)(2,1)S(1)}, bf16[432,128]{1,0:T(8,128)(2,1)S(1)}) custom-call(s32[4]{0:T(128)S(1)} %pad_add_fusion.scal_ref, bf16[384,128]{1,0:T(8,128)(2,1)S(1)} %collective-permute-done.5.qa_ref, bf16[384,128]{1,0:T(8,128)(2,1)S(1)} %collective-permute-done.6.qb_ref, bf16[8,912,128]{2,1,0:T(8,128)(2,1)S(1)} %all-to-all-done.came_ref), custom_call_target="tpu_custom_call" | custom-call | tf_op jit(solution)/shard_map/attention/pallas_call | solution.py:207
  53.5 0.9 collective-permute-start.14
  54.8 1.3 %collective-permute-start.16 = (bf16[384,640]{1,0:T(8,128)(2,1)S(1)}, bf16[384,640]{1,0:T(8,128)(2,1)S(1)}, u32[]{:S(2)}, u32[]{:S(2)}) collective-permute-start(bf16[384,640]{1,0:T(8,128)(2,1)S(1)} %get-tuple-element.68), channel_id=1, source_target_pairs={{0,3},{1,2},{2,1},{3,0},{4,7},{5,6},{6,5},{7,4},{8,11},{9,10},{10,... | collective-permute-start | bytes 1474568 | tf_op jit(solution)/shard_map/ppermute | solution.py:333
  56.1 1.6 %collective-permute-start.7 = (bf16[432,128]{1,0:T(8,128)(2,1)S(1)}, bf16[432,128]{1,0:T(8,128)(2,1)S(1)}, u32[]{:S(2)}, u32[]{:S(2)}) collective-permute-start(bf16[432,128]{1,0:T(8,128)(2,1)S(1)} %get-tuple-element.43), channel_id=1, source_target_pairs={{0,4},{4,8},{8,12},{12,16},{16,20},{20,24},{24,28},{28,0},{1,5},{5... | collective-permute-start | bytes 331784 | tf_op jit(solution)/shard_map/ppermute | solution.py:315
  57.7 3.9 %collective-permute-start.8 = (bf16[432,128]{1,0:T(8,128)(2,1)S(1)}, bf16[432,128]{1,0:T(8,128)(2,1)S(1)}, u32[]{:S(2)}, u32[]{:S(2)}) collective-permute-start(bf16[432,128]{1,0:T(8,128)(2,1)S(1)} %get-tuple-element.44), channel_id=1, source_target_pairs={{0,28},{4,0},{8,4},{12,8},{16,12},{20,16},{24,20},{28,24},{1,29},{... | collective-permute-start | bytes 331784 | tf_op jit(solution)/shard_map/ppermute | solution.py:315
  61.7 1.6 %attention.5 = (f32[432,128]{1,0:T(8,128)S(1)}, f32[432,128]{1,0:T(8,128)S(1)}) custom-call(s32[4]{0:T(128)S(1)} %pad_add_fusion.scal_ref, bf16[384,128]{1,0:T(8,128)(2,1)S(1)} %collective-permute-done.3.qa_ref, bf16[384,128]{1,0:T(8,128)(2,1)S(1)} %collective-permute-done.4.qb_ref, bf16[8,912,128]{2,1,0:T(8,128)(2,1)S(1)} %all-to-all-done.came_ref), custom_call_target="tpu_custom_call" | custom-call | tf_op jit(solution)/shard_map/attention/pallas_call | solution.py:207
  63.2 1.7 %collective-permute-done.7.refs_0_ = bf16[432,128]{1,0:T(8,128)(2,1)S(1)} collective-permute-done((bf16[432,128]{1,0:T(8,128)(2,1)S(1)}, bf16[432,128]{1,0:T(8,128)(2,1)S(1)}, u32[]{:S(2)}, u32[]{:S(2)}) %collective-permute-start.7) | collective-permute-done | bytes 110624 | tf_op jit(solution)/shard_map/ppermute | solution.py:315
  65.1 2.7 %collective-permute-start.10 = (bf16[432,128]{1,0:T(8,128)(2,1)S(1)}, bf16[432,128]{1,0:T(8,128)(2,1)S(1)}, u32[]{:S(2)}, u32[]{:S(2)}) collective-permute-start(bf16[432,128]{1,0:T(8,128)(2,1)S(1)} %get-tuple-element.50), channel_id=1, source_target_pairs={{0,28},{4,0},{8,4},{12,8},{16,12},{20,16},{24,20},{28,24},{1,29},{... | collective-permute-start | bytes 331784 | tf_op jit(solution)/shard_map/ppermute | solution.py:315
  67.8 1.6 %attention.6 = (f32[432,128]{1,0:T(8,128)S(1)}, f32[432,128]{1,0:T(8,128)S(1)}) custom-call(s32[4]{0:T(128)S(1)} %pad_add_fusion.scal_ref, bf16[384,128]{1,0:T(8,128)(2,1)S(1)} %collective-permute-done.1.qa_ref, bf16[384,128]{1,0:T(8,128)(2,1)S(1)} %collective-permute-done.2.qb_ref, bf16[8,912,128]{2,1,0:T(8,128)(2,1)S(1)} %all-to-all-done.came_ref), custom_call_target="tpu_custom_call" | custom-call | tf_op jit(solution)/shard_map/attention/pallas_call | solution.py:207
  70.0 2.7 %collective-permute-start.12 = (bf16[432,128]{1,0:T(8,128)(2,1)S(1)}, bf16[432,128]{1,0:T(8,128)(2,1)S(1)}, u32[]{:S(2)}, u32[]{:S(2)}) collective-permute-start(bf16[432,128]{1,0:T(8,128)(2,1)S(1)} %get-tuple-element.56), channel_id=1, source_target_pairs={{0,28},{4,0},{8,4},{12,8},{16,12},{20,16},{24,20},{28,24},{1,29},{... | collective-permute-start | bytes 331784 | tf_op jit(solution)/shard_map/ppermute | solution.py:315
  72.7 1.6 %attention.7 = (f32[432,128]{1,0:T(8,128)S(1)}, f32[432,128]{1,0:T(8,128)S(1)}) custom-call(s32[4]{0:T(128)S(1)} %pad_add_fusion.scal_ref, bf16[384,128]{1,0:T(8,128)(2,1)S(1)} %get-tuple-element.57.qa_ref, bf16[384,128]{1,0:T(8,128)(2,1)S(1)} %collective-permute-done.qb_ref, bf16[8,912,128]{2,1,0:T(8,128)(2,1)S(1)} %all-to-all-done.came_ref), custom_call_target="tpu_custom_call" | custom-call | tf_op jit(solution)/shard_map/attention/pallas_call | solution.py:207
  74.5 3.1 %collective-permute-start.13 = (bf16[432,128]{1,0:T(8,128)(2,1)S(1)}, bf16[432,128]{1,0:T(8,128)(2,1)S(1)}, u32[]{:S(2)}, u32[]{:S(2)}) collective-permute-start(bf16[432,128]{1,0:T(8,128)(2,1)S(1)} %joined.5), channel_id=1, source_target_pairs={{0,28},{4,0},{8,4},{12,8},{16,12},{20,16},{24,20},{28,24},{1,29},{... | collective-permute-start | bytes 331784 | tf_op jit(solution)/shard_map/ppermute | solution.py:315
  77.8 1.3 %collective-permute-done.11.up_ref = bf16[432,128]{1,0:T(8,128)(2,1)S(1)} collective-permute-done((bf16[432,128]{1,0:T(8,128)(2,1)S(1)}, bf16[432,128]{1,0:T(8,128)(2,1)S(1)}, u32[]{:S(2)}, u32[]{:S(2)}) %collective-permute-start.11) | collective-permute-done | bytes 110624 | tf_op jit(solution)/shard_map/ppermute | solution.py:315
  79.6 10.3 %all-gather.1 = bf16[576,384]{1,0:T(8,128)(2,1)S(1)} all-gather(bf16[144,384]{1,0:T(8,128)(2,1)S(1)} %get-tuple-element.63), channel_id=3, replica_groups=mesh['yh'=2,'x'=4,'z'=8,'yl'=2,'core'=2] {'yl','core'}, dimensions={0}, use_global_device_ids=true | all-gather | bytes 552960 | tf_op jit(solution)/shard_map/all_gather | solution.py:369
  89.9 2.1 %finish.1 = (bf16[128,640]{1,0:T(8,128)(2,1)}, bf16[2,640]{1,0:T(2,128)(2,1)}) custom-call(s32[4]{0:T(128)S(1)} %pad_add_fusion.scal_ref, bf16[4,144,384]{2,1,0:T(8,128)(2,1)S(1)} %bitcast.10, bf16[384,640]{1,0:T(8,128)(2,1)S(1)} %collective-permute-done.14.w1_ref, bf16[384,640]{1,0:T(8,128)(2,1)S(1)} %collective-permute-done.15.w2_ref, ...), custom_call_target="tpu_custom_call" | custom-call | tf_op jit(solution)/shard_map/finish/pallas_call | solution.py:297
  (35 shorter events, 3.6 us)
Async XLA Ops:
  2.0 1.2 %copy-start.3 = (bf16[256,3,640]{2,0,1:T(8,128)(2,1)S(1)}, bf16[256,3,640]{2,0,1:T(8,128)(2,1)}, u32[]{:S(2)}) copy-start(bf16[256,3,640]{2,0,1:T(8,128)(2,1)} %param.13) | copy-start | bytes 2949124
  3.2 1.1 %copy-start.4 = (bf16[128,2560]{1,0:T(8,128)(2,1)S(1)}, bf16[128,2560]{1,0:T(8,128)(2,1)}, u32[]{:S(2)}) copy-start(bf16[128,2560]{1,0:T(8,128)(2,1)} %lat_ref.1) | copy-start | bytes 1966084
  4.3 0.7 copy-start.6
  5.0 0.7 copy-start.7
  15.0 2.7 %copy-start.1 = (bf16[2560,3,384]{2,0,1:T(8,128)(2,1)S(1)}, bf16[2560,3,384]{2,0,1:T(8,128)(2,1)}, u32[]{:S(2)}) copy-start(bf16[2560,3,384]{2,0,1:T(8,128)(2,1)} %param.14) | copy-start | bytes 17694724
  19.4 1.3 %copy-start.2 = (bf16[8,912,128]{2,1,0:T(8,128)(2,1)}, bf16[8,912,128]{2,1,0:T(8,128)(2,1)S(1)}, u32[]{:S(2)}) copy-start(bf16[8,912,128]{2,1,0:T(8,128)(2,1)S(1)} %get-tuple-element.38) | copy-start | bytes 5603332
  20.7 31.1 %all-to-all-start = ((bf16[8,912,128]{2,1,0:T(8,128)(2,1)}), bf16[8,912,128]{2,1,0:T(8,128)(2,1)S(1)}, u32[]{:S(2)}, u32[]{:S(2)}) async-start(bf16[8,912,128]{2,1,0:T(8,128)(2,1)} %copy-done.2), calls=%async_computation | async-start | bytes 3735552 | tf_op jit(solution)/shard_map/all_to_all | solution.py:354
  25.6 8.4 %collective-permute-start = (bf16[384,128]{1,0:T(8,128)(2,1)S(1)}, bf16[384,128]{1,0:T(8,128)(2,1)S(1)}, u32[]{:S(2)}, u32[]{:S(2)}) collective-permute-start(bf16[384,128]{1,0:T(8,128)(2,1)S(1)} %get-tuple-element.57.qa_ref), channel_id=1, source_target_pairs={{0,4},{4,8},{8,12},{12,16},{16,20},{20,24},{24,28},{28,0},{1,5},{5... | collective-permute-start | bytes 294920 | tf_op jit(solution)/shard_map/ppermute | solution.py:315
  27.2 6.7 %collective-permute-start.1 = (bf16[384,128]{1,0:T(8,128)(2,1)S(1)}, bf16[384,128]{1,0:T(8,128)(2,1)S(1)}, u32[]{:S(2)}, u32[]{:S(2)}) collective-permute-start(bf16[384,128]{1,0:T(8,128)(2,1)S(1)} %get-tuple-element.57.qa_ref), channel_id=1, source_target_pairs={{0,28},{4,0},{8,4},{12,8},{16,12},{20,16},{24,20},{28,24},{1,29},{... | collective-permute-start | bytes 294920 | tf_op jit(solution)/shard_map/ppermute | solution.py:315
  33.9 5.0 %collective-permute-start.2 = (bf16[384,128]{1,0:T(8,128)(2,1)S(1)}, bf16[384,128]{1,0:T(8,128)(2,1)S(1)}, u32[]{:S(2)}, u32[]{:S(2)}) collective-permute-start(bf16[384,128]{1,0:T(8,128)(2,1)S(1)} %collective-permute-done.qb_ref), channel_id=1, source_target_pairs={{0,4},{4,8},{8,12},{12,16},{16,20},{20,24},{24,28},{28,0},{1,5},{5... | collective-permute-start | bytes 294920 | tf_op jit(solution)/shard_map/ppermute | solution.py:315
  33.9 5.0 %collective-permute-start.3 = (bf16[384,128]{1,0:T(8,128)(2,1)S(1)}, bf16[384,128]{1,0:T(8,128)(2,1)S(1)}, u32[]{:S(2)}, u32[]{:S(2)}) collective-permute-start(bf16[384,128]{1,0:T(8,128)(2,1)S(1)} %collective-permute-done.1.qa_ref), channel_id=1, source_target_pairs={{0,28},{4,0},{8,4},{12,8},{16,12},{20,16},{24,20},{28,24},{1,29},{... | collective-permute-start | bytes 294920 | tf_op jit(solution)/shard_map/ppermute | solution.py:315
  38.9 5.0 %collective-permute-start.4 = (bf16[384,128]{1,0:T(8,128)(2,1)S(1)}, bf16[384,128]{1,0:T(8,128)(2,1)S(1)}, u32[]{:S(2)}, u32[]{:S(2)}) collective-permute-start(bf16[384,128]{1,0:T(8,128)(2,1)S(1)} %collective-permute-done.2.qb_ref), channel_id=1, source_target_pairs={{0,4},{4,8},{8,12},{12,16},{16,20},{20,24},{24,28},{28,0},{1,5},{5... | collective-permute-start | bytes 294920 | tf_op jit(solution)/shard_map/ppermute | solution.py:315
  38.9 5.0 %collective-permute-start.5 = (bf16[384,128]{1,0:T(8,128)(2,1)S(1)}, bf16[384,128]{1,0:T(8,128)(2,1)S(1)}, u32[]{:S(2)}, u32[]{:S(2)}) collective-permute-start(bf16[384,128]{1,0:T(8,128)(2,1)S(1)} %collective-permute-done.3.qa_ref), channel_id=1, source_target_pairs={{0,28},{4,0},{8,4},{12,8},{16,12},{20,16},{24,20},{28,24},{1,29},{... | collective-permute-start | bytes 294920 | tf_op jit(solution)/shard_map/ppermute | solution.py:315
  43.9 5.0 %collective-permute-start.6 = (bf16[384,128]{1,0:T(8,128)(2,1)S(1)}, bf16[384,128]{1,0:T(8,128)(2,1)S(1)}, u32[]{:S(2)}, u32[]{:S(2)}) collective-permute-start(bf16[384,128]{1,0:T(8,128)(2,1)S(1)} %collective-permute-done.4.qb_ref), channel_id=1, source_target_pairs={{0,4},{4,8},{8,12},{12,16},{16,20},{20,24},{24,28},{28,0},{1,5},{5... | collective-permute-start | bytes 294920 | tf_op jit(solution)/shard_map/ppermute | solution.py:315
  51.8 1.6 %copy-start = (bf16[384,2560]{1,0:T(8,128)(2,1)S(1)}, bf16[384,2560]{1,0:T(8,128)(2,1)}, u32[]{:S(2)}) copy-start(bf16[384,2560]{1,0:T(8,128)(2,1)} %w_ref.1) | copy-start | bytes 5898244
  53.5 24.1 %collective-permute-start.14 = (bf16[384,640]{1,0:T(8,128)(2,1)S(1)}, bf16[384,640]{1,0:T(8,128)(2,1)S(1)}, u32[]{:S(2)}, u32[]{:S(2)}) collective-permute-start(bf16[384,640]{1,0:T(8,128)(2,1)S(1)} %get-tuple-element.70), channel_id=1, source_target_pairs={{0,1},{1,0},{2,3},{3,2},{4,5},{5,4},{6,7},{7,6},{8,9},{9,8},{10,11... | collective-permute-start | bytes 1474568 | tf_op jit(solution)/shard_map/ppermute | solution.py:333
  54.3 23.3 %collective-permute-start.15 = (bf16[384,640]{1,0:T(8,128)(2,1)S(1)}, bf16[384,640]{1,0:T(8,128)(2,1)S(1)}, u32[]{:S(2)}, u32[]{:S(2)}) collective-permute-start(bf16[384,640]{1,0:T(8,128)(2,1)S(1)} %get-tuple-element.69), channel_id=1, source_target_pairs={{0,2},{1,3},{2,0},{3,1},{4,6},{5,7},{6,4},{7,5},{8,10},{9,11},{10,... | collective-permute-start | bytes 1474568 | tf_op jit(solution)/shard_map/ppermute | solution.py:333
  54.8 23.1 %collective-permute-start.16 = (bf16[384,640]{1,0:T(8,128)(2,1)S(1)}, bf16[384,640]{1,0:T(8,128)(2,1)S(1)}, u32[]{:S(2)}, u32[]{:S(2)}) collective-permute-start(bf16[384,640]{1,0:T(8,128)(2,1)S(1)} %get-tuple-element.68), channel_id=1, source_target_pairs={{0,3},{1,2},{2,1},{3,0},{4,7},{5,6},{6,5},{7,4},{8,11},{9,10},{10,... | collective-permute-start | bytes 1474568 | tf_op jit(solution)/shard_map/ppermute | solution.py:333
  56.1 8.9 %collective-permute-start.7 = (bf16[432,128]{1,0:T(8,128)(2,1)S(1)}, bf16[432,128]{1,0:T(8,128)(2,1)S(1)}, u32[]{:S(2)}, u32[]{:S(2)}) collective-permute-start(bf16[432,128]{1,0:T(8,128)(2,1)S(1)} %get-tuple-element.43), channel_id=1, source_target_pairs={{0,4},{4,8},{8,12},{12,16},{16,20},{20,24},{24,28},{28,0},{1,5},{5... | collective-permute-start | bytes 331784 | tf_op jit(solution)/shard_map/ppermute | solution.py:315
  57.7 7.2 %collective-permute-start.8 = (bf16[432,128]{1,0:T(8,128)(2,1)S(1)}, bf16[432,128]{1,0:T(8,128)(2,1)S(1)}, u32[]{:S(2)}, u32[]{:S(2)}) collective-permute-start(bf16[432,128]{1,0:T(8,128)(2,1)S(1)} %get-tuple-element.44), channel_id=1, source_target_pairs={{0,28},{4,0},{8,4},{12,8},{16,12},{20,16},{24,20},{28,24},{1,29},{... | collective-permute-start | bytes 331784 | tf_op jit(solution)/shard_map/ppermute | solution.py:315
  65.0 4.9 %collective-permute-start.9 = (bf16[432,128]{1,0:T(8,128)(2,1)S(1)}, bf16[432,128]{1,0:T(8,128)(2,1)S(1)}, u32[]{:S(2)}, u32[]{:S(2)}) collective-permute-start(bf16[432,128]{1,0:T(8,128)(2,1)S(1)} %get-tuple-element.49), channel_id=1, source_target_pairs={{0,4},{4,8},{8,12},{12,16},{16,20},{20,24},{24,28},{28,0},{1,5},{5... | collective-permute-start | bytes 331784 | tf_op jit(solution)/shard_map/ppermute | solution.py:315
  65.1 4.8 %collective-permute-start.10 = (bf16[432,128]{1,0:T(8,128)(2,1)S(1)}, bf16[432,128]{1,0:T(8,128)(2,1)S(1)}, u32[]{:S(2)}, u32[]{:S(2)}) collective-permute-start(bf16[432,128]{1,0:T(8,128)(2,1)S(1)} %get-tuple-element.50), channel_id=1, source_target_pairs={{0,28},{4,0},{8,4},{12,8},{16,12},{20,16},{24,20},{28,24},{1,29},{... | collective-permute-start | bytes 331784 | tf_op jit(solution)/shard_map/ppermute | solution.py:315
  69.9 20.0 %copy-start.5 = (bf16[128,640]{1,0:T(8,128)(2,1)S(1)}, bf16[128,640]{1,0:T(8,128)(2,1)}, u32[]{:S(2)}) copy-start(bf16[128,640]{1,0:T(8,128)(2,1)} %fresh_ref.1) | copy-start | bytes 491524
  70.0 4.5 %collective-permute-start.12 = (bf16[432,128]{1,0:T(8,128)(2,1)S(1)}, bf16[432,128]{1,0:T(8,128)(2,1)S(1)}, u32[]{:S(2)}, u32[]{:S(2)}) collective-permute-start(bf16[432,128]{1,0:T(8,128)(2,1)S(1)} %get-tuple-element.56), channel_id=1, source_target_pairs={{0,28},{4,0},{8,4},{12,8},{16,12},{20,16},{24,20},{28,24},{1,29},{... | collective-permute-start | bytes 331784 | tf_op jit(solution)/shard_map/ppermute | solution.py:315
  74.3 4.9 %collective-permute-start.11 = (bf16[432,128]{1,0:T(8,128)(2,1)S(1)}, bf16[432,128]{1,0:T(8,128)(2,1)S(1)}, u32[]{:S(2)}, u32[]{:S(2)}) collective-permute-start(bf16[432,128]{1,0:T(8,128)(2,1)S(1)} %get-tuple-element.55), channel_id=1, source_target_pairs={{0,4},{4,8},{8,12},{12,16},{16,20},{20,24},{24,28},{28,0},{1,5},{5... | collective-permute-start | bytes 331784 | tf_op jit(solution)/shard_map/ppermute | solution.py:315
  74.5 4.9 %collective-permute-start.13 = (bf16[432,128]{1,0:T(8,128)(2,1)S(1)}, bf16[432,128]{1,0:T(8,128)(2,1)S(1)}, u32[]{:S(2)}, u32[]{:S(2)}) collective-permute-start(bf16[432,128]{1,0:T(8,128)(2,1)S(1)} %joined.5), channel_id=1, source_target_pairs={{0,28},{4,0},{8,4},{12,8},{16,12},{20,16},{24,20},{28,24},{1,29},{... | collective-permute-start | bytes 331784 | tf_op jit(solution)/shard_map/ppermute | solution.py:315

commit v3 on v2

--- a/solution.py
+++ b/solution.py
@@ -30,6 +30,9 @@
 TURNS = ((6, 7), (4, 5), (2, 3), (0, 1))
 
 
+LONG = pl.CostEstimate(flops=10_000_000_000, transcendentals=0, bytes_accessed=20_000_000)
+
+
 def vmem(n):
     return [pl.BlockSpec(memory_space=pltpu.VMEM)] * n
 
@@ -54,18 +57,33 @@
     return lax.dot_general(a, b, (((1,), (1,)), ((), ())), preferred_element_type=F32)
 
 
-def opening_kernel(
-    level_ref, scal_ref, ada_ref, lat_ref, qg_ref, kg_ref, mod_ref, normed_ref, own_ref
-):
+def embedding_kernel(level_ref, out_ref):
     half = 128
     index = lax.broadcasted_iota(jnp.int32, (16, 2 * half), 1)
     place = jnp.where(index < half, index, index - half).astype(F32)
     frequency = jnp.exp(-math.log(10000.0) * place / half)
     angle = level_ref[0].astype(F32) * frequency
     wave = jnp.where(index < half, jnp.cos(angle), jnp.sin(angle))
-    embedding = (wave * (1.0 / (1.0 + jnp.exp(-wave)))).astype(BF16)
+    out_ref[...] = (wave * (1.0 / (1.0 + jnp.exp(-wave)))).astype(BF16)
+
+
+def embedded(levels):
+    return pl.pallas_call(
+        embedding_kernel,
+        out_shape=jax.ShapeDtypeStruct((16, 256), BF16),
+        in_specs=[smem()],
+        out_specs=vmem(1)[0],
+        compiler_params=params(16),
+        cost_estimate=LONG,
+        name="embedding",
+    )(levels)
+
+
+def opening_kernel(
+    emb_ref, scal_ref, ada_ref, lat_ref, qg_ref, kg_ref, mod_ref, normed_ref, own_ref
+):
     for j in range(3):
-        mod_ref[pl.ds(j, 1), :] = dot(embedding, ada_ref[j])[0:1]
+        mod_ref[pl.ds(j, 1), :] = dot(emb_ref[...], ada_ref[j])[0:1]
     mod_ref[3:4, 0:HD] = qg_ref[...]
     mod_ref[4:5, 0:HD] = kg_ref[...]
     states = lat_ref[...].astype(F32)
@@ -73,12 +91,12 @@
     centered = states - average
     variance = jnp.mean(centered * centered, axis=-1, keepdims=True)
     normed_ref[...] = centered * lax.rsqrt(variance + 1e-06)
-    first = pl.multiple_of(scal_ref[3] * QW, 128)
+    first = pl.multiple_of(scal_ref[2] * QW, 128)
     for k in range(5):
         own_ref[:, k * 128 : (k + 1) * 128] = lat_ref[:, pl.ds(first + k * 128, 128)]
 
 
-def opening(levels, scal, ada, latents, q_gain, k_gain):
+def opening(embedding, scal, ada, latents, q_gain, k_gain):
     return pl.pallas_call(
         opening_kernel,
         out_shape=(
@@ -86,11 +104,12 @@
             jax.ShapeDtypeStruct((ROWS, D), F32),
             jax.ShapeDtypeStruct((ROWS, QW), BF16),
         ),
-        in_specs=[smem(), smem()] + vmem(4),
+        in_specs=vmem(1) + [smem()] + vmem(4),
         out_specs=tuple(vmem(3)),
         compiler_params=params(16),
+        cost_estimate=LONG,
         name="opening",
-    )(levels, scal, ada, latents, q_gain, k_gain)
+    )(embedding, scal, ada, latents, q_gain, k_gain)
 
 
 def rms_rounded(matrix, gain, factor):
@@ -158,8 +177,8 @@
     )(normed, mods, mod, own, w)
 
 
-def attention_kernel(slots, scal_ref, qa_ref, qb_ref, came_ref, *out_refs):
-    column, line, oldest = scal_ref[0], scal_ref[1], scal_ref[2]
+def attention_kernel(slots, scal_ref, slot_ref, qa_ref, qb_ref, came_ref, *out_refs):
+    column, line, oldest = scal_ref[0], scal_ref[1], slot_ref[0]
     key_block = lax.broadcasted_iota(jnp.int32, (1, COLS * ROWS), 1) // ROWS
     key_rank = (key_block * LINE + line - oldest) & (BLOCKS - 1)
     ranks, places = [], []
@@ -202,16 +221,16 @@
     return jnp.concatenate([high, totals - high], axis=0)
 
 
-def partial_attention(scal, slots, queries, came, kind):
+def partial_attention(scal, head_slot, slots, queries, came, kind):
     shape = jax.ShapeDtypeStruct((RETURN, HD), kind)
     return pl.pallas_call(
         functools.partial(attention_kernel, slots),
         out_shape=(shape, shape),
-        in_specs=[smem()] + vmem(3),
+        in_specs=[smem(), smem()] + vmem(3),
         out_specs=tuple(vmem(2)),
         compiler_params=params(16),
         name="attention",
-    )(scal, *[queries[slot] for slot in slots], came)
+    )(scal, head_slot, *[queries[slot] for slot in slots], came)
 
 
 def joined_kernel(*refs):
@@ -264,15 +283,16 @@
         in_specs=vmem(3),
         out_specs=tuple(vmem(2)),
         compiler_params=params(16),
+        cost_estimate=LONG,
         name="combine",
     )(up, down, own)
 
 
 def finish_kernel(
-    scal_ref, att_ref, w1_ref, w2_ref, w3_ref, own_ref, mod_ref, leaving_ref, fresh_ref, w_ref,
+    scal_ref, slot_ref, att_ref, w1_ref, w2_ref, w3_ref, own_ref, mod_ref, leaving_ref, fresh_ref, w_ref,
     window_ref, clean_ref, w_held, sem,
 ):
-    tensor = scal_ref[3]
+    tensor = scal_ref[2]
     first = pl.multiple_of(tensor * QW, 128)
     copy = pltpu.make_async_copy(w_ref.at[:, pl.ds(first, QW)], w_held, sem)
     copy.start()
@@ -281,7 +301,7 @@
     projected = projected + dot(att_ref[tensor ^ 3], w3_ref[...])
     copy.wait()
     projected = projected + dot(att_ref[tensor], w_held[...])
-    oldest = scal_ref[0] * LINE + scal_ref[1] == scal_ref[2]
+    oldest = scal_ref[0] * LINE + scal_ref[1] == slot_ref[0]
     leaving = leaving_ref[...]
     for k in range(5):
         at = slice(k * 128, (k + 1) * 128)
@@ -293,19 +313,19 @@
         clean_ref[:, at] = (old + gate * projected[ROWS : ROWS + 2, at]).astype(BF16)
 
 
-def finish(scal, attended, pieces, own, mod, leaving, fresh, w):
+def finish(scal, head_slot, attended, pieces, own, mod, leaving, fresh, w):
     return pl.pallas_call(
         finish_kernel,
         out_shape=(
             jax.ShapeDtypeStruct((ROWS, QW), BF16),
             jax.ShapeDtypeStruct((2, QW), BF16),
         ),
-        in_specs=[smem()] + vmem(8) + [hbm()],
+        in_specs=[smem(), smem()] + vmem(8) + [hbm()],
         out_specs=tuple(vmem(2)),
         scratch_shapes=[pltpu.VMEM((QROWS, QW), BF16), pltpu.SemaphoreType.DMA],
         compiler_params=params(16),
         name="finish",
-    )(scal, attended, *pieces, own, mod, leaving, fresh, w)
+    )(scal, head_slot, attended, *pieces, own, mod, leaving, fresh, w)
 
 
 COLUMN, TENSOR = ("yh", "x"), ("yl", "core")
@@ -342,32 +362,32 @@
 def local(
     latents, levels, head_slot, fresh_noise, ada_weight, qkv_weight, q_gain, k_gain, out_weight
 ):
-    oldest = head_slot[0]
     scal = jnp.stack(
-        [lax.axis_index(COLUMN), lax.axis_index("z"), oldest, lax.axis_index(TENSOR)]
+        [lax.axis_index(COLUMN), lax.axis_index("z"), lax.axis_index(TENSOR)]
     ).astype(jnp.int32)
     ada = jnp.transpose(ada_weight, (1, 0, 2))
     w = jnp.transpose(qkv_weight, (1, 0, 2))
-    mod, normed, own = opening(levels, scal, ada, latents, q_gain[None], k_gain[None])
+    mod, normed, own = opening(
+        embedded(levels), scal, ada, latents, q_gain[None], k_gain[None]
+    )
     mods = lax.all_gather(mod, TENSOR, axis=0, tiled=False)
     q, sent = front(normed, mods, mod, own, w)
     came = lax.all_to_all(sent, COLUMN, 0, 0)
     queries = ring(q)
     came, *queries = lax.optimization_barrier((came, *queries))
-    up, down = partial_attention(scal, TURNS[0], queries, came, BF16)
+    up, down = partial_attention(scal, head_slot, TURNS[0], queries, came, BF16)
     weights = exchanged(out_weight, down)
     for turn in (1, 2):
         up, down = shifted(up, 1), shifted(down, -1)
-        up, down = joined(
-            (up, down), partial_attention(scal, TURNS[turn], queries, came, F32)
-        )
+        parts = partial_attention(scal, head_slot, TURNS[turn], queries, came, F32)
+        up, down = joined((up, down), parts)
     up, down = shifted(up, 1), shifted(down, -1)
-    still, last = partial_attention(scal, TURNS[3], queries, came, F32)
+    still, last = partial_attention(scal, head_slot, TURNS[3], queries, came, F32)
     still, weights = lax.optimization_barrier((still, weights))
     down = shifted(joined((down,), (last,))[0], -1)
     attended, leaving = combine(up, down, still)
     attended = lax.all_gather(attended, TENSOR, axis=0, tiled=False)
-    return finish(scal, attended, weights, own, mod, leaving, fresh_noise, out_weight)
+    return finish(scal, head_slot, attended, weights, own, mod, leaving, fresh_noise, out_weight)
 
 
 def solution(mesh):

time: 92.5 us -> 86.9 us (0.939)
  local copies, waits for them, and re-layouts: 7.66 us -> 2.6 us
    unnamed x16 -> x18, local copies, waits for them, and re-layouts: 7.52 us -> 2.46 us
  transfers between devices with their start and end apart: 18 -> 18, of which waited for: 11 -> 11; matrix products, arithmetic and copies ran while one was open for 0% -> 0% of each run, Pallas kernels for 5% -> 6%
where the time goes in v3:
time: 86.9 us; the launch traced here: 86.6 us
  starting transfers between devices  32.8 us (38%)
  blocking collectives  18.6 us (21%)
  waiting for transfers between devices  18.6 us (21%)
  Pallas kernels  11.6 us (13%)
  local copies, waits for them, and re-layouts  2.6 us (3%)
  between operations  2.28 us (3%)
    ppermute x14, starting transfers between devices, shifted(): lax.ppermute(array, 'z', [(i, (i + step) % LINE) for i in range(LINE)])  25.3 us
    ppermute x14, waiting for transfers between devices, shifted(): lax.ppermute(array, 'z', [(i, (i + step) % LINE) for i in range(LINE)])  15.5 us
    all_gather x1, blocking collectives, local(): attended = lax.all_gather(attended, TENSOR, axis=0, tiled=False)  10.3 us
    all_gather x1, blocking collectives, local(): mods = lax.all_gather(mod, TENSOR, axis=0, tiled=False)  8.36 us
    pallas_call x4, Pallas kernels, partial_attention(): pl.pallas_call(functools.partial(attention_kernel, slots), out_shape=(sha...  6.27 us
    all_to_all x1, starting transfers between devices, local(): came = lax.all_to_all(sent, COLUMN, 0, 0)  4.91 us
    all_to_all x1, waiting for transfers between devices, local(): came = lax.all_to_all(sent, COLUMN, 0, 0)  2.9 us
    ppermute x3, starting transfers between devices, exchanged(): lax.ppermute(lax.dynamic_slice_in_dim(weight, (place ^ d) * QW, QW, 1), T...  2.59 us
  transfers between devices with their start and end apart: 18, of which 11 were waited for; matrix products, arithmetic and copies ran while one was open for 0% of the time, Pallas kernels for 6%

profile of v3, /device:TPU:1, one launch (start us, length us, event | category | flops | bytes accessed | tf_op | source)
XLA Modules:
  0.0 86.6 jit_solution(11642641174548585257)
XLA Ops:
  1.5 1.0 %copy-done.3 = bf16[256,3,640]{2,0,1:T(8,128)(2,1)S(1)} copy-done((bf16[256,3,640]{2,0,1:T(8,128)(2,1)S(1)}, bf16[256,3,640]{2,0,1:T(8,128)(2,1)}, u32[]{:S(2)}) %copy-start.3) | copy-done | bytes 983064
  2.7 1.0 %opening.1 = (f32[8,640]{1,0:T(8,128)S(1)}, f32[128,2560]{1,0:T(8,128)S(1)}, bf16[128,640]{1,0:T(8,128)(2,1)S(1)}) custom-call(bf16[16,256]{1,0:T(8,128)(2,1)S(1)} %embedding.1.emb_ref, s32[3]{0:T(128)S(1)} %pad_add_fusion.scal_ref, bf16[3,256,640]{2,1,0:T(8,128)(2,1)S(1)} %bitcast.14, bf16[128,2560]{1,0:T(8,128)(2,1)S(1)} %copy-done.4, ...), custom_call_target="tpu_custom_call" | custom-call | flops 10000000000 | bytes 20000000 | tf_op jit(solution)/shard_map/opening/pallas_call | solution.py:100
  3.7 8.4 %all-gather = f32[32,640]{1,0:T(8,128)S(1)} all-gather(f32[8,640]{1,0:T(8,128)S(1)} %get-tuple-element.36.mod_ref), channel_id=2, replica_groups=mesh['yh'=2,'x'=4,'z'=8,'yl'=2,'core'=2] {'yl','core'}, dimensions={0}, use_global_device_ids=true | all-gather | bytes 102400 | tf_op jit(solution)/shard_map/all_gather | solution.py:373
  12.1 1.8 %front.1 = (bf16[384,128]{1,0:T(8,128)(2,1)S(1)}, bf16[8,912,128]{2,1,0:T(8,128)(2,1)S(1)}) custom-call(f32[128,2560]{1,0:T(8,128)S(1)} %get-tuple-element.35.normed_ref, f32[4,8,640]{2,1,0:T(8,128)S(1)} %bitcast.13, f32[8,640]{1,0:T(8,128)S(1)} %get-tuple-element.36.mod_ref, bf16[128,640]{1,0:T(8,128)(2,1)S(1)} %get-tuple-element.37.own_ref, ...), custom_call_target="tpu_custom_call" | custom-call | tf_op jit(solution)/shard_map/front/pallas_call | solution.py:162
  13.9 1.3 %copy-done.1 = bf16[8,912,128]{2,1,0:T(8,128)(2,1)} copy-done((bf16[8,912,128]{2,1,0:T(8,128)(2,1)}, bf16[8,912,128]{2,1,0:T(8,128)(2,1)S(1)}, u32[]{:S(2)}) %copy-start.1) | copy-done | bytes 1867800
  15.2 4.9 %all-to-all-start = ((bf16[8,912,128]{2,1,0:T(8,128)(2,1)}), bf16[8,912,128]{2,1,0:T(8,128)(2,1)S(1)}, u32[]{:S(2)}, u32[]{:S(2)}) async-start(bf16[8,912,128]{2,1,0:T(8,128)(2,1)} %copy-done.1), calls=%async_computation | async-start | bytes 3735552 | tf_op jit(solution)/shard_map/all_to_all | solution.py:375
  20.1 1.6 %collective-permute-start = (bf16[384,128]{1,0:T(8,128)(2,1)S(1)}, bf16[384,128]{1,0:T(8,128)(2,1)S(1)}, u32[]{:S(2)}, u32[]{:S(2)}) collective-permute-start(bf16[384,128]{1,0:T(8,128)(2,1)S(1)} %get-tuple-element.57.qa_ref), channel_id=1, source_target_pairs={{0,4},{4,8},{8,12},{12,16},{16,20},{20,24},{24,28},{28,0},{1,5},{5... | collective-permute-start | bytes 294920 | tf_op jit(solution)/shard_map/ppermute | solution.py:335
  21.7 4.0 %collective-permute-start.1 = (bf16[384,128]{1,0:T(8,128)(2,1)S(1)}, bf16[384,128]{1,0:T(8,128)(2,1)S(1)}, u32[]{:S(2)}, u32[]{:S(2)}) collective-permute-start(bf16[384,128]{1,0:T(8,128)(2,1)S(1)} %get-tuple-element.57.qa_ref), channel_id=1, source_target_pairs={{0,28},{4,0},{8,4},{12,8},{16,12},{20,16},{24,20},{28,24},{1,29},{... | collective-permute-start | bytes 294920 | tf_op jit(solution)/shard_map/ppermute | solution.py:335
  25.7 2.7 %collective-permute-done.qb_ref = bf16[384,128]{1,0:T(8,128)(2,1)S(1)} collective-permute-done((bf16[384,128]{1,0:T(8,128)(2,1)S(1)}, bf16[384,128]{1,0:T(8,128)(2,1)S(1)}, u32[]{:S(2)}, u32[]{:S(2)}) %collective-permute-start) | collective-permute-done | bytes 98336 | tf_op jit(solution)/shard_map/ppermute | solution.py:335
  28.4 2.7 %collective-permute-start.3 = (bf16[384,128]{1,0:T(8,128)(2,1)S(1)}, bf16[384,128]{1,0:T(8,128)(2,1)S(1)}, u32[]{:S(2)}, u32[]{:S(2)}) collective-permute-start(bf16[384,128]{1,0:T(8,128)(2,1)S(1)} %collective-permute-done.1.qa_ref), channel_id=1, source_target_pairs={{0,28},{4,0},{8,4},{12,8},{16,12},{20,16},{24,20},{28,24},{1,29},{... | collective-permute-start | bytes 294920 | tf_op jit(solution)/shard_map/ppermute | solution.py:335
  31.1 2.3 %collective-permute-done.2.qb_ref = bf16[384,128]{1,0:T(8,128)(2,1)S(1)} collective-permute-done((bf16[384,128]{1,0:T(8,128)(2,1)S(1)}, bf16[384,128]{1,0:T(8,128)(2,1)S(1)}, u32[]{:S(2)}, u32[]{:S(2)}) %collective-permute-start.2) | collective-permute-done | bytes 98336 | tf_op jit(solution)/shard_map/ppermute | solution.py:335
  33.4 2.7 %collective-permute-start.5 = (bf16[384,128]{1,0:T(8,128)(2,1)S(1)}, bf16[384,128]{1,0:T(8,128)(2,1)S(1)}, u32[]{:S(2)}, u32[]{:S(2)}) collective-permute-start(bf16[384,128]{1,0:T(8,128)(2,1)S(1)} %collective-permute-done.3.qa_ref), channel_id=1, source_target_pairs={{0,28},{4,0},{8,4},{12,8},{16,12},{20,16},{24,20},{28,24},{1,29},{... | collective-permute-start | bytes 294920 | tf_op jit(solution)/shard_map/ppermute | solution.py:335
  36.1 2.3 %collective-permute-done.4.qb_ref = bf16[384,128]{1,0:T(8,128)(2,1)S(1)} collective-permute-done((bf16[384,128]{1,0:T(8,128)(2,1)S(1)}, bf16[384,128]{1,0:T(8,128)(2,1)S(1)}, u32[]{:S(2)}, u32[]{:S(2)}) %collective-permute-start.4) | collective-permute-done | bytes 98336 | tf_op jit(solution)/shard_map/ppermute | solution.py:335
  39.0 4.3 %collective-permute-done.6.qb_ref = bf16[384,128]{1,0:T(8,128)(2,1)S(1)} collective-permute-done((bf16[384,128]{1,0:T(8,128)(2,1)S(1)}, bf16[384,128]{1,0:T(8,128)(2,1)S(1)}, u32[]{:S(2)}, u32[]{:S(2)}) %collective-permute-start.6) | collective-permute-done | bytes 98336 | tf_op jit(solution)/shard_map/ppermute | solution.py:335
  43.3 2.9 %all-to-all-done.came_ref = bf16[8,912,128]{2,1,0:T(8,128)(2,1)S(1)} async-done(((bf16[8,912,128]{2,1,0:T(8,128)(2,1)}), bf16[8,912,128]{2,1,0:T(8,128)(2,1)S(1)}, u32[]{:S(2)}, u32[]{:S(2)}) %all-to-all-start) | async-done | bytes 1867808 | tf_op jit(solution)/shard_map/all_to_all | solution.py:375
  46.2 1.6 %attention.4 = (bf16[432,128]{1,0:T(8,128)(2,1)S(1)}, bf16[432,128]{1,0:T(8,128)(2,1)S(1)}) custom-call(s32[3]{0:T(128)S(1)} %pad_add_fusion.scal_ref, s32[1]{0:T(128)S(6)} %copy.12.slot_ref, bf16[384,128]{1,0:T(8,128)(2,1)S(1)} %collective-permute-done.5.qa_ref, bf16[384,128]{1,0:T(8,128)(2,1)S(1)} %collective-permute-done.6.qb_ref, ...), custom_call_target="tpu_custom_call" | custom-call | tf_op jit(solution)/shard_map/attention/pallas_call | solution.py:226
  48.0 0.9 collective-permute-start.14
  48.8 0.4 collective-permute-start.15
  49.2 1.3 %collective-permute-start.16 = (bf16[384,640]{1,0:T(8,128)(2,1)S(1)}, bf16[384,640]{1,0:T(8,128)(2,1)S(1)}, u32[]{:S(2)}, u32[]{:S(2)}) collective-permute-start(bf16[384,640]{1,0:T(8,128)(2,1)S(1)} %get-tuple-element.68), channel_id=1, source_target_pairs={{0,3},{1,2},{2,1},{3,0},{4,7},{5,6},{6,5},{7,4},{8,11},{9,10},{10,... | collective-permute-start | bytes 1474568 | tf_op jit(solution)/shard_map/ppermute | solution.py:353
  50.5 1.6 %collective-permute-start.7 = (bf16[432,128]{1,0:T(8,128)(2,1)S(1)}, bf16[432,128]{1,0:T(8,128)(2,1)S(1)}, u32[]{:S(2)}, u32[]{:S(2)}) collective-permute-start(bf16[432,128]{1,0:T(8,128)(2,1)S(1)} %get-tuple-element.43), channel_id=1, source_target_pairs={{0,4},{4,8},{8,12},{12,16},{16,20},{20,24},{24,28},{28,0},{1,5},{5... | collective-permute-start | bytes 331784 | tf_op jit(solution)/shard_map/ppermute | solution.py:335
  52.2 3.9 %collective-permute-start.8 = (bf16[432,128]{1,0:T(8,128)(2,1)S(1)}, bf16[432,128]{1,0:T(8,128)(2,1)S(1)}, u32[]{:S(2)}, u32[]{:S(2)}) collective-permute-start(bf16[432,128]{1,0:T(8,128)(2,1)S(1)} %get-tuple-element.44), channel_id=1, source_target_pairs={{0,28},{4,0},{8,4},{12,8},{16,12},{20,16},{24,20},{28,24},{1,29},{... | collective-permute-start | bytes 331784 | tf_op jit(solution)/shard_map/ppermute | solution.py:335
  56.1 1.6 %attention.5 = (f32[432,128]{1,0:T(8,128)S(1)}, f32[432,128]{1,0:T(8,128)S(1)}) custom-call(s32[3]{0:T(128)S(1)} %pad_add_fusion.scal_ref, s32[1]{0:T(128)S(6)} %copy.12.slot_ref, bf16[384,128]{1,0:T(8,128)(2,1)S(1)} %collective-permute-done.3.qa_ref, bf16[384,128]{1,0:T(8,128)(2,1)S(1)} %collective-permute-done.4.qb_ref, ...), custom_call_target="tpu_custom_call" | custom-call | tf_op jit(solution)/shard_map/attention/pallas_call | solution.py:226
  57.7 1.7 %collective-permute-done.7.refs_0_ = bf16[432,128]{1,0:T(8,128)(2,1)S(1)} collective-permute-done((bf16[432,128]{1,0:T(8,128)(2,1)S(1)}, bf16[432,128]{1,0:T(8,128)(2,1)S(1)}, u32[]{:S(2)}, u32[]{:S(2)}) %collective-permute-start.7) | collective-permute-done | bytes 110624 | tf_op jit(solution)/shard_map/ppermute | solution.py:335
  59.6 2.7 %collective-permute-start.10 = (bf16[432,128]{1,0:T(8,128)(2,1)S(1)}, bf16[432,128]{1,0:T(8,128)(2,1)S(1)}, u32[]{:S(2)}, u32[]{:S(2)}) collective-permute-start(bf16[432,128]{1,0:T(8,128)(2,1)S(1)} %get-tuple-element.50), channel_id=1, source_target_pairs={{0,28},{4,0},{8,4},{12,8},{16,12},{20,16},{24,20},{28,24},{1,29},{... | collective-permute-start | bytes 331784 | tf_op jit(solution)/shard_map/ppermute | solution.py:335
  62.2 1.6 %attention.6 = (f32[432,128]{1,0:T(8,128)S(1)}, f32[432,128]{1,0:T(8,128)S(1)}) custom-call(s32[3]{0:T(128)S(1)} %pad_add_fusion.scal_ref, s32[1]{0:T(128)S(6)} %copy.12.slot_ref, bf16[384,128]{1,0:T(8,128)(2,1)S(1)} %collective-permute-done.1.qa_ref, bf16[384,128]{1,0:T(8,128)(2,1)S(1)} %collective-permute-done.2.qb_ref, ...), custom_call_target="tpu_custom_call" | custom-call | tf_op jit(solution)/shard_map/attention/pallas_call | solution.py:226
  63.8 0.6 collective-permute-done.9.refs_0_
  64.4 2.7 %collective-permute-start.12 = (bf16[432,128]{1,0:T(8,128)(2,1)S(1)}, bf16[432,128]{1,0:T(8,128)(2,1)S(1)}, u32[]{:S(2)}, u32[]{:S(2)}) collective-permute-start(bf16[432,128]{1,0:T(8,128)(2,1)S(1)} %get-tuple-element.56), channel_id=1, source_target_pairs={{0,28},{4,0},{8,4},{12,8},{16,12},{20,16},{24,20},{28,24},{1,29},{... | collective-permute-start | bytes 331784 | tf_op jit(solution)/shard_map/ppermute | solution.py:335
  67.2 1.6 %attention.7 = (f32[432,128]{1,0:T(8,128)S(1)}, f32[432,128]{1,0:T(8,128)S(1)}) custom-call(s32[3]{0:T(128)S(1)} %pad_add_fusion.scal_ref, s32[1]{0:T(128)S(6)} %copy.12.slot_ref, bf16[384,128]{1,0:T(8,128)(2,1)S(1)} %get-tuple-element.57.qa_ref, bf16[384,128]{1,0:T(8,128)(2,1)S(1)} %collective-permute-done.qb_ref, ...), custom_call_target="tpu_custom_call" | custom-call | tf_op jit(solution)/shard_map/attention/pallas_call | solution.py:226
  69.0 3.1 %collective-permute-start.13 = (bf16[432,128]{1,0:T(8,128)(2,1)S(1)}, bf16[432,128]{1,0:T(8,128)(2,1)S(1)}, u32[]{:S(2)}, u32[]{:S(2)}) collective-permute-start(bf16[432,128]{1,0:T(8,128)(2,1)S(1)} %joined.5), channel_id=1, source_target_pairs={{0,28},{4,0},{8,4},{12,8},{16,12},{20,16},{24,20},{28,24},{1,29},{... | collective-permute-start | bytes 331784 | tf_op jit(solution)/shard_map/ppermute | solution.py:335
  72.3 1.3 %collective-permute-done.11.up_ref = bf16[432,128]{1,0:T(8,128)(2,1)S(1)} collective-permute-done((bf16[432,128]{1,0:T(8,128)(2,1)S(1)}, bf16[432,128]{1,0:T(8,128)(2,1)S(1)}, u32[]{:S(2)}, u32[]{:S(2)}) %collective-permute-start.11) | collective-permute-done | bytes 110624 | tf_op jit(solution)/shard_map/ppermute | solution.py:335
  74.1 10.3 %all-gather.1 = bf16[576,384]{1,0:T(8,128)(2,1)S(1)} all-gather(bf16[144,384]{1,0:T(8,128)(2,1)S(1)} %get-tuple-element.63), channel_id=3, replica_groups=mesh['yh'=2,'x'=4,'z'=8,'yl'=2,'core'=2] {'yl','core'}, dimensions={0}, use_global_device_ids=true | all-gather | bytes 552960 | tf_op jit(solution)/shard_map/all_gather | solution.py:389
  84.4 2.1 %finish.1 = (bf16[128,640]{1,0:T(8,128)(2,1)}, bf16[2,640]{1,0:T(2,128)(2,1)}) custom-call(s32[3]{0:T(128)S(1)} %pad_add_fusion.scal_ref, s32[1]{0:T(128)S(6)} %copy.12.slot_ref, bf16[4,144,384]{2,1,0:T(8,128)(2,1)S(1)} %bitcast.12, bf16[384,640]{1,0:T(8,128)(2,1)S(1)} %collective-permute-done.14.w1_ref, ...), custom_call_target="tpu_custom_call" | custom-call | tf_op jit(solution)/shard_map/finish/pallas_call | solution.py:317
  (39 shorter events, 1.6 us)
Async XLA Ops:
  1.3 1.2 %copy-start.3 = (bf16[256,3,640]{2,0,1:T(8,128)(2,1)S(1)}, bf16[256,3,640]{2,0,1:T(8,128)(2,1)}, u32[]{:S(2)}) copy-start(bf16[256,3,640]{2,0,1:T(8,128)(2,1)} %param.13) | copy-start | bytes 2949124
  1.3 1.4 %copy-start.4 = (bf16[128,2560]{1,0:T(8,128)(2,1)S(1)}, bf16[128,2560]{1,0:T(8,128)(2,1)}, u32[]{:S(2)}) copy-start(bf16[128,2560]{1,0:T(8,128)(2,1)} %lat_ref.1) | copy-start | bytes 1966084
  1.3 1.4 %copy-start.5 = (f32[128]{0:T(128)S(1)}, f32[128]{0:T(128)}, u32[]{:S(2)}) copy-start(f32[128]{0:T(128)} %param.15) | copy-start | bytes 1540
  1.3 1.4 %copy-start.6 = (f32[128]{0:T(128)S(1)}, f32[128]{0:T(128)}, u32[]{:S(2)}) copy-start(f32[128]{0:T(128)} %param.16) | copy-start | bytes 1540
  1.5 10.6 %slice-start = ((s8[5898240]{0:T(1024)(128)(4,1)}), s8[4194304]{0:T(1024)(128)(4,1)S(1)}, s32[]{:S(2)}) async-start(s8[5898240]{0:T(1024)(128)(4,1)} %bitcast.9), calls=%async_computation.1 | async-start | bytes 8388608
  2.7 9.4 %slice-start.1 = ((s8[5898240]{0:T(1024)(128)(4,1)}), s8[1703936]{0:T(1024)(128)(4,1)S(1)}, s32[]{:S(2)}) async-start(s8[5898240]{0:T(1024)(128)(4,1)} %bitcast.9), calls=%async_computation.2 | async-start | bytes 3407872
  13.9 1.3 %copy-start.1 = (bf16[8,912,128]{2,1,0:T(8,128)(2,1)}, bf16[8,912,128]{2,1,0:T(8,128)(2,1)S(1)}, u32[]{:S(2)}) copy-start(bf16[8,912,128]{2,1,0:T(8,128)(2,1)S(1)} %get-tuple-element.38) | copy-start | bytes 5603332
  15.2 31.1 %all-to-all-start = ((bf16[8,912,128]{2,1,0:T(8,128)(2,1)}), bf16[8,912,128]{2,1,0:T(8,128)(2,1)S(1)}, u32[]{:S(2)}, u32[]{:S(2)}) async-start(bf16[8,912,128]{2,1,0:T(8,128)(2,1)} %copy-done.1), calls=%async_computation | async-start | bytes 3735552 | tf_op jit(solution)/shard_map/all_to_all | solution.py:375
  20.1 8.3 %collective-permute-start = (bf16[384,128]{1,0:T(8,128)(2,1)S(1)}, bf16[384,128]{1,0:T(8,128)(2,1)S(1)}, u32[]{:S(2)}, u32[]{:S(2)}) collective-permute-start(bf16[384,128]{1,0:T(8,128)(2,1)S(1)} %get-tuple-element.57.qa_ref), channel_id=1, source_target_pairs={{0,4},{4,8},{8,12},{12,16},{16,20},{20,24},{24,28},{28,0},{1,5},{5... | collective-permute-start | bytes 294920 | tf_op jit(solution)/shard_map/ppermute | solution.py:335
  21.7 6.7 %collective-permute-start.1 = (bf16[384,128]{1,0:T(8,128)(2,1)S(1)}, bf16[384,128]{1,0:T(8,128)(2,1)S(1)}, u32[]{:S(2)}, u32[]{:S(2)}) collective-permute-start(bf16[384,128]{1,0:T(8,128)(2,1)S(1)} %get-tuple-element.57.qa_ref), channel_id=1, source_target_pairs={{0,28},{4,0},{8,4},{12,8},{16,12},{20,16},{24,20},{28,24},{1,29},{... | collective-permute-start | bytes 294920 | tf_op jit(solution)/shard_map/ppermute | solution.py:335
  28.4 5.0 %collective-permute-start.2 = (bf16[384,128]{1,0:T(8,128)(2,1)S(1)}, bf16[384,128]{1,0:T(8,128)(2,1)S(1)}, u32[]{:S(2)}, u32[]{:S(2)}) collective-permute-start(bf16[384,128]{1,0:T(8,128)(2,1)S(1)} %collective-permute-done.qb_ref), channel_id=1, source_target_pairs={{0,4},{4,8},{8,12},{12,16},{16,20},{20,24},{24,28},{28,0},{1,5},{5... | collective-permute-start | bytes 294920 | tf_op jit(solution)/shard_map/ppermute | solution.py:335
  28.4 5.0 %collective-permute-start.3 = (bf16[384,128]{1,0:T(8,128)(2,1)S(1)}, bf16[384,128]{1,0:T(8,128)(2,1)S(1)}, u32[]{:S(2)}, u32[]{:S(2)}) collective-permute-start(bf16[384,128]{1,0:T(8,128)(2,1)S(1)} %collective-permute-done.1.qa_ref), channel_id=1, source_target_pairs={{0,28},{4,0},{8,4},{12,8},{16,12},{20,16},{24,20},{28,24},{1,29},{... | collective-permute-start | bytes 294920 | tf_op jit(solution)/shard_map/ppermute | solution.py:335
  33.4 5.0 %collective-permute-start.4 = (bf16[384,128]{1,0:T(8,128)(2,1)S(1)}, bf16[384,128]{1,0:T(8,128)(2,1)S(1)}, u32[]{:S(2)}, u32[]{:S(2)}) collective-permute-start(bf16[384,128]{1,0:T(8,128)(2,1)S(1)} %collective-permute-done.2.qb_ref), channel_id=1, source_target_pairs={{0,4},{4,8},{8,12},{12,16},{16,20},{20,24},{24,28},{28,0},{1,5},{5... | collective-permute-start | bytes 294920 | tf_op jit(solution)/shard_map/ppermute | solution.py:335
  33.4 5.6 %collective-permute-start.5 = (bf16[384,128]{1,0:T(8,128)(2,1)S(1)}, bf16[384,128]{1,0:T(8,128)(2,1)S(1)}, u32[]{:S(2)}, u32[]{:S(2)}) collective-permute-start(bf16[384,128]{1,0:T(8,128)(2,1)S(1)} %collective-permute-done.3.qa_ref), channel_id=1, source_target_pairs={{0,28},{4,0},{8,4},{12,8},{16,12},{20,16},{24,20},{28,24},{1,29},{... | collective-permute-start | bytes 294920 | tf_op jit(solution)/shard_map/ppermute | solution.py:335
  38.4 5.0 %collective-permute-start.6 = (bf16[384,128]{1,0:T(8,128)(2,1)S(1)}, bf16[384,128]{1,0:T(8,128)(2,1)S(1)}, u32[]{:S(2)}, u32[]{:S(2)}) collective-permute-start(bf16[384,128]{1,0:T(8,128)(2,1)S(1)} %collective-permute-done.4.qb_ref), channel_id=1, source_target_pairs={{0,4},{4,8},{8,12},{12,16},{16,20},{20,24},{24,28},{28,0},{1,5},{5... | collective-permute-start | bytes 294920 | tf_op jit(solution)/shard_map/ppermute | solution.py:335
  46.2 1.6 %copy-start = (bf16[384,2560]{1,0:T(8,128)(2,1)S(1)}, bf16[384,2560]{1,0:T(8,128)(2,1)}, u32[]{:S(2)}) copy-start(bf16[384,2560]{1,0:T(8,128)(2,1)} %w_ref.1) | copy-start | bytes 5898244
  48.0 24.1 %collective-permute-start.14 = (bf16[384,640]{1,0:T(8,128)(2,1)S(1)}, bf16[384,640]{1,0:T(8,128)(2,1)S(1)}, u32[]{:S(2)}, u32[]{:S(2)}) collective-permute-start(bf16[384,640]{1,0:T(8,128)(2,1)S(1)} %get-tuple-element.70), channel_id=1, source_target_pairs={{0,1},{1,0},{2,3},{3,2},{4,5},{5,4},{6,7},{7,6},{8,9},{9,8},{10,11... | collective-permute-start | bytes 1474568 | tf_op jit(solution)/shard_map/ppermute | solution.py:353
  48.8 23.3 %collective-permute-start.15 = (bf16[384,640]{1,0:T(8,128)(2,1)S(1)}, bf16[384,640]{1,0:T(8,128)(2,1)S(1)}, u32[]{:S(2)}, u32[]{:S(2)}) collective-permute-start(bf16[384,640]{1,0:T(8,128)(2,1)S(1)} %get-tuple-element.69), channel_id=1, source_target_pairs={{0,2},{1,3},{2,0},{3,1},{4,6},{5,7},{6,4},{7,5},{8,10},{9,11},{10,... | collective-permute-start | bytes 1474568 | tf_op jit(solution)/shard_map/ppermute | solution.py:353
  49.2 23.1 %collective-permute-start.16 = (bf16[384,640]{1,0:T(8,128)(2,1)S(1)}, bf16[384,640]{1,0:T(8,128)(2,1)S(1)}, u32[]{:S(2)}, u32[]{:S(2)}) collective-permute-start(bf16[384,640]{1,0:T(8,128)(2,1)S(1)} %get-tuple-element.68), channel_id=1, source_target_pairs={{0,3},{1,2},{2,1},{3,0},{4,7},{5,6},{6,5},{7,4},{8,11},{9,10},{10,... | collective-permute-start | bytes 1474568 | tf_op jit(solution)/shard_map/ppermute | solution.py:353
  50.5 8.9 %collective-permute-start.7 = (bf16[432,128]{1,0:T(8,128)(2,1)S(1)}, bf16[432,128]{1,0:T(8,128)(2,1)S(1)}, u32[]{:S(2)}, u32[]{:S(2)}) collective-permute-start(bf16[432,128]{1,0:T(8,128)(2,1)S(1)} %get-tuple-element.43), channel_id=1, source_target_pairs={{0,4},{4,8},{8,12},{12,16},{16,20},{20,24},{24,28},{28,0},{1,5},{5... | collective-permute-start | bytes 331784 | tf_op jit(solution)/shard_map/ppermute | solution.py:335
  52.2 7.2 %collective-permute-start.8 = (bf16[432,128]{1,0:T(8,128)(2,1)S(1)}, bf16[432,128]{1,0:T(8,128)(2,1)S(1)}, u32[]{:S(2)}, u32[]{:S(2)}) collective-permute-start(bf16[432,128]{1,0:T(8,128)(2,1)S(1)} %get-tuple-element.44), channel_id=1, source_target_pairs={{0,28},{4,0},{8,4},{12,8},{16,12},{20,16},{24,20},{28,24},{1,29},{... | collective-permute-start | bytes 331784 | tf_op jit(solution)/shard_map/ppermute | solution.py:335
  59.5 4.9 %collective-permute-start.9 = (bf16[432,128]{1,0:T(8,128)(2,1)S(1)}, bf16[432,128]{1,0:T(8,128)(2,1)S(1)}, u32[]{:S(2)}, u32[]{:S(2)}) collective-permute-start(bf16[432,128]{1,0:T(8,128)(2,1)S(1)} %get-tuple-element.49), channel_id=1, source_target_pairs={{0,4},{4,8},{8,12},{12,16},{16,20},{20,24},{24,28},{28,0},{1,5},{5... | collective-permute-start | bytes 331784 | tf_op jit(solution)/shard_map/ppermute | solution.py:335
  59.6 4.8 %collective-permute-start.10 = (bf16[432,128]{1,0:T(8,128)(2,1)S(1)}, bf16[432,128]{1,0:T(8,128)(2,1)S(1)}, u32[]{:S(2)}, u32[]{:S(2)}) collective-permute-start(bf16[432,128]{1,0:T(8,128)(2,1)S(1)} %get-tuple-element.50), channel_id=1, source_target_pairs={{0,28},{4,0},{8,4},{12,8},{16,12},{20,16},{24,20},{28,24},{1,29},{... | collective-permute-start | bytes 331784 | tf_op jit(solution)/shard_map/ppermute | solution.py:335
  64.4 4.5 %collective-permute-start.12 = (bf16[432,128]{1,0:T(8,128)(2,1)S(1)}, bf16[432,128]{1,0:T(8,128)(2,1)S(1)}, u32[]{:S(2)}, u32[]{:S(2)}) collective-permute-start(bf16[432,128]{1,0:T(8,128)(2,1)S(1)} %get-tuple-element.56), channel_id=1, source_target_pairs={{0,28},{4,0},{8,4},{12,8},{16,12},{20,16},{24,20},{28,24},{1,29},{... | collective-permute-start | bytes 331784 | tf_op jit(solution)/shard_map/ppermute | solution.py:335
  68.8 4.9 %collective-permute-start.11 = (bf16[432,128]{1,0:T(8,128)(2,1)S(1)}, bf16[432,128]{1,0:T(8,128)(2,1)S(1)}, u32[]{:S(2)}, u32[]{:S(2)}) collective-permute-start(bf16[432,128]{1,0:T(8,128)(2,1)S(1)} %get-tuple-element.55), channel_id=1, source_target_pairs={{0,4},{4,8},{8,12},{12,16},{16,20},{20,24},{24,28},{28,0},{1,5},{5... | collective-permute-start | bytes 331784 | tf_op jit(solution)/shard_map/ppermute | solution.py:335
  69.0 4.9 %collective-permute-start.13 = (bf16[432,128]{1,0:T(8,128)(2,1)S(1)}, bf16[432,128]{1,0:T(8,128)(2,1)S(1)}, u32[]{:S(2)}, u32[]{:S(2)}) collective-permute-start(bf16[432,128]{1,0:T(8,128)(2,1)S(1)} %joined.5), channel_id=1, source_target_pairs={{0,28},{4,0},{8,4},{12,8},{16,12},{20,16},{24,20},{28,24},{1,29},{... | collective-permute-start | bytes 331784 | tf_op jit(solution)/shard_map/ppermute | solution.py:335
  72.3 12.1 %copy-start.2 = (bf16[128,640]{1,0:T(8,128)(2,1)S(1)}, bf16[128,640]{1,0:T(8,128)(2,1)}, u32[]{:S(2)}) copy-start(bf16[128,640]{1,0:T(8,128)(2,1)} %fresh_ref.1) | copy-start | bytes 491524

commit v4 on v3

--- a/solution.py
+++ b/solution.py
@@ -289,18 +289,13 @@
 
 
 def finish_kernel(
-    scal_ref, slot_ref, att_ref, w1_ref, w2_ref, w3_ref, own_ref, mod_ref, leaving_ref, fresh_ref, w_ref,
-    window_ref, clean_ref, w_held, sem,
+    scal_ref, slot_ref, att_ref, w0_ref, w1_ref, w2_ref, w3_ref, own_ref, mod_ref, leaving_ref,
+    fresh_ref, window_ref, clean_ref,
 ):
     tensor = scal_ref[2]
-    first = pl.multiple_of(tensor * QW, 128)
-    copy = pltpu.make_async_copy(w_ref.at[:, pl.ds(first, QW)], w_held, sem)
-    copy.start()
-    projected = dot(att_ref[tensor ^ 1], w1_ref[...])
-    projected = projected + dot(att_ref[tensor ^ 2], w2_ref[...])
-    projected = projected + dot(att_ref[tensor ^ 3], w3_ref[...])
-    copy.wait()
-    projected = projected + dot(att_ref[tensor], w_held[...])
+    projected = dot(att_ref[tensor], w0_ref[...])
+    for d, w_ref in enumerate((w1_ref, w2_ref, w3_ref), 1):
+        projected = projected + dot(att_ref[tensor ^ d], w_ref[...])
     oldest = scal_ref[0] * LINE + scal_ref[1] == slot_ref[0]
     leaving = leaving_ref[...]
     for k in range(5):
@@ -313,19 +308,18 @@
         clean_ref[:, at] = (old + gate * projected[ROWS : ROWS + 2, at]).astype(BF16)
 
 
-def finish(scal, head_slot, attended, pieces, own, mod, leaving, fresh, w):
+def finish(scal, head_slot, attended, pieces, own, mod, leaving, fresh):
     return pl.pallas_call(
         finish_kernel,
         out_shape=(
             jax.ShapeDtypeStruct((ROWS, QW), BF16),
             jax.ShapeDtypeStruct((2, QW), BF16),
         ),
-        in_specs=[smem(), smem()] + vmem(8) + [hbm()],
+        in_specs=[smem(), smem()] + vmem(9),
         out_specs=tuple(vmem(2)),
-        scratch_shapes=[pltpu.VMEM((QROWS, QW), BF16), pltpu.SemaphoreType.DMA],
         compiler_params=params(16),
         name="finish",
-    )(scal, head_slot, attended, *pieces, own, mod, leaving, fresh, w)
+    )(scal, head_slot, attended, *pieces, own, mod, leaving, fresh)
 
 
 COLUMN, TENSOR = ("yh", "x"), ("yl", "core")
@@ -349,13 +343,11 @@
 def exchanged(weight, after):
     place = lax.axis_index(TENSOR)
     weight, _ = lax.optimization_barrier((weight, after))
-    return [
-        lax.ppermute(
-            lax.dynamic_slice_in_dim(weight, (place ^ d) * QW, QW, 1),
-            TENSOR,
-            [(i, i ^ d) for i in range(4)],
-        )
-        for d in (1, 2, 3)
+    parts = [
+        lax.dynamic_slice_in_dim(weight, (place ^ d) * QW, QW, 1) for d in range(4)
+    ]
+    return parts[:1] + [
+        lax.ppermute(parts[d], TENSOR, [(i, i ^ d) for i in range(4)]) for d in (1, 2, 3)
     ]
 
 
@@ -387,7 +379,7 @@
     down = shifted(joined((down,), (last,))[0], -1)
     attended, leaving = combine(up, down, still)
     attended = lax.all_gather(attended, TENSOR, axis=0, tiled=False)
-    return finish(scal, head_slot, attended, weights, own, mod, leaving, fresh_noise, out_weight)
+    return finish(scal, head_slot, attended, weights, own, mod, leaving, fresh_noise)
 
 
 def solution(mesh):

time: 86.9 us -> 86.5 us (level)
  no operation moved by 1% of the time
where the time goes in v4:
time: 86.5 us; the launch traced here: 86.2 us
  starting transfers between devices  32.8 us (38%)
  blocking collectives  18.6 us (22%)
  waiting for transfers between devices  18.6 us (22%)
  Pallas kernels  11.4 us (13%)
  local copies, waits for them, and re-layouts  2.64 us (3%)
  between operations  2.12 us (2%)
    ppermute x14, starting transfers between devices, shifted(): lax.ppermute(array, 'z', [(i, (i + step) % LINE) for i in range(LINE)])  25.3 us
    ppermute x14, waiting for transfers between devices, shifted(): lax.ppermute(array, 'z', [(i, (i + step) % LINE) for i in range(LINE)])  15.4 us
    all_gather x1, blocking collectives, local(): attended = lax.all_gather(attended, TENSOR, axis=0, tiled=False)  10.3 us
    all_gather x1, blocking collectives, local(): mods = lax.all_gather(mod, TENSOR, axis=0, tiled=False)  8.36 us
    pallas_call x4, Pallas kernels, partial_attention(): pl.pallas_call(functools.partial(attention_kernel, slots), out_shape=(sha...  6.27 us
    all_to_all x1, starting transfers between devices, local(): came = lax.all_to_all(sent, COLUMN, 0, 0)  4.91 us
    all_to_all x1, waiting for transfers between devices, local(): came = lax.all_to_all(sent, COLUMN, 0, 0)  2.9 us
    ppermute x3, starting transfers between devices, exchanged(): lax.ppermute(parts[d], TENSOR, [(i, i ^ d) for i in range(4)])  2.59 us
  transfers between devices with their start and end apart: 18, of which 11 were waited for; matrix products, arithmetic and copies ran while one was open for 0% of the time, Pallas kernels for 6%

profile of v4, /device:TPU:1, one launch (start us, length us, event | category | flops | bytes accessed | tf_op | source)
XLA Modules:
  0.0 86.2 jit_solution(12044477062776629195)
XLA Ops:
  1.5 1.0 %copy-done.2 = bf16[256,3,640]{2,0,1:T(8,128)(2,1)S(1)} copy-done((bf16[256,3,640]{2,0,1:T(8,128)(2,1)S(1)}, bf16[256,3,640]{2,0,1:T(8,128)(2,1)}, u32[]{:S(2)}) %copy-start.2) | copy-done | bytes 983064
  2.7 1.0 %opening.1 = (f32[8,640]{1,0:T(8,128)S(1)}, f32[128,2560]{1,0:T(8,128)S(1)}, bf16[128,640]{1,0:T(8,128)(2,1)S(1)}) custom-call(bf16[16,256]{1,0:T(8,128)(2,1)S(1)} %embedding.1.emb_ref, s32[3]{0:T(128)S(1)} %pad_add_fusion.scal_ref, bf16[3,256,640]{2,1,0:T(8,128)(2,1)S(1)} %bitcast.14, bf16[128,2560]{1,0:T(8,128)(2,1)S(1)} %copy-done.3, ...), custom_call_target="tpu_custom_call" | custom-call | flops 10000000000 | bytes 20000000 | tf_op jit(solution)/shard_map/opening/pallas_call | solution.py:100
  3.7 8.4 %all-gather = f32[32,640]{1,0:T(8,128)S(1)} all-gather(f32[8,640]{1,0:T(8,128)S(1)} %get-tuple-element.37.mod_ref), channel_id=2, replica_groups=mesh['yh'=2,'x'=4,'z'=8,'yl'=2,'core'=2] {'yl','core'}, dimensions={0}, use_global_device_ids=true | all-gather | bytes 102400 | tf_op jit(solution)/shard_map/all_gather | solution.py:365
  12.1 1.8 %front.1 = (bf16[384,128]{1,0:T(8,128)(2,1)S(1)}, bf16[8,912,128]{2,1,0:T(8,128)(2,1)S(1)}) custom-call(f32[128,2560]{1,0:T(8,128)S(1)} %get-tuple-element.36.normed_ref, f32[4,8,640]{2,1,0:T(8,128)S(1)} %bitcast.13, f32[8,640]{1,0:T(8,128)S(1)} %get-tuple-element.37.mod_ref, bf16[128,640]{1,0:T(8,128)(2,1)S(1)} %get-tuple-element.38.own_ref, ...), custom_call_target="tpu_custom_call" | custom-call | tf_op jit(solution)/shard_map/front/pallas_call | solution.py:162
  13.9 1.3 %copy-done = bf16[8,912,128]{2,1,0:T(8,128)(2,1)} copy-done((bf16[8,912,128]{2,1,0:T(8,128)(2,1)}, bf16[8,912,128]{2,1,0:T(8,128)(2,1)S(1)}, u32[]{:S(2)}) %copy-start) | copy-done | bytes 1867800
  15.2 4.9 %all-to-all-start = ((bf16[8,912,128]{2,1,0:T(8,128)(2,1)}), bf16[8,912,128]{2,1,0:T(8,128)(2,1)S(1)}, u32[]{:S(2)}, u32[]{:S(2)}) async-start(bf16[8,912,128]{2,1,0:T(8,128)(2,1)} %copy-done), calls=%async_computation | async-start | bytes 3735552 | tf_op jit(solution)/shard_map/all_to_all | solution.py:367
  20.1 1.6 %collective-permute-start = (bf16[384,128]{1,0:T(8,128)(2,1)S(1)}, bf16[384,128]{1,0:T(8,128)(2,1)S(1)}, u32[]{:S(2)}, u32[]{:S(2)}) collective-permute-start(bf16[384,128]{1,0:T(8,128)(2,1)S(1)} %get-tuple-element.58.qa_ref), channel_id=1, source_target_pairs={{0,4},{4,8},{8,12},{12,16},{16,20},{20,24},{24,28},{28,0},{1,5},{5... | collective-permute-start | bytes 294920 | tf_op jit(solution)/shard_map/ppermute | solution.py:329
  21.7 4.0 %collective-permute-start.1 = (bf16[384,128]{1,0:T(8,128)(2,1)S(1)}, bf16[384,128]{1,0:T(8,128)(2,1)S(1)}, u32[]{:S(2)}, u32[]{:S(2)}) collective-permute-start(bf16[384,128]{1,0:T(8,128)(2,1)S(1)} %get-tuple-element.58.qa_ref), channel_id=1, source_target_pairs={{0,28},{4,0},{8,4},{12,8},{16,12},{20,16},{24,20},{28,24},{1,29},{... | collective-permute-start | bytes 294920 | tf_op jit(solution)/shard_map/ppermute | solution.py:329
  25.7 2.7 %collective-permute-done.qb_ref = bf16[384,128]{1,0:T(8,128)(2,1)S(1)} collective-permute-done((bf16[384,128]{1,0:T(8,128)(2,1)S(1)}, bf16[384,128]{1,0:T(8,128)(2,1)S(1)}, u32[]{:S(2)}, u32[]{:S(2)}) %collective-permute-start) | collective-permute-done | bytes 98336 | tf_op jit(solution)/shard_map/ppermute | solution.py:329
  28.4 2.7 %collective-permute-start.3 = (bf16[384,128]{1,0:T(8,128)(2,1)S(1)}, bf16[384,128]{1,0:T(8,128)(2,1)S(1)}, u32[]{:S(2)}, u32[]{:S(2)}) collective-permute-start(bf16[384,128]{1,0:T(8,128)(2,1)S(1)} %collective-permute-done.1.qa_ref), channel_id=1, source_target_pairs={{0,28},{4,0},{8,4},{12,8},{16,12},{20,16},{24,20},{28,24},{1,29},{... | collective-permute-start | bytes 294920 | tf_op jit(solution)/shard_map/ppermute | solution.py:329
  31.1 2.3 %collective-permute-done.2.qb_ref = bf16[384,128]{1,0:T(8,128)(2,1)S(1)} collective-permute-done((bf16[384,128]{1,0:T(8,128)(2,1)S(1)}, bf16[384,128]{1,0:T(8,128)(2,1)S(1)}, u32[]{:S(2)}, u32[]{:S(2)}) %collective-permute-start.2) | collective-permute-done | bytes 98336 | tf_op jit(solution)/shard_map/ppermute | solution.py:329
  33.4 2.7 %collective-permute-start.5 = (bf16[384,128]{1,0:T(8,128)(2,1)S(1)}, bf16[384,128]{1,0:T(8,128)(2,1)S(1)}, u32[]{:S(2)}, u32[]{:S(2)}) collective-permute-start(bf16[384,128]{1,0:T(8,128)(2,1)S(1)} %collective-permute-done.3.qa_ref), channel_id=1, source_target_pairs={{0,28},{4,0},{8,4},{12,8},{16,12},{20,16},{24,20},{28,24},{1,29},{... | collective-permute-start | bytes 294920 | tf_op jit(solution)/shard_map/ppermute | solution.py:329
  36.1 2.3 %collective-permute-done.4.qb_ref = bf16[384,128]{1,0:T(8,128)(2,1)S(1)} collective-permute-done((bf16[384,128]{1,0:T(8,128)(2,1)S(1)}, bf16[384,128]{1,0:T(8,128)(2,1)S(1)}, u32[]{:S(2)}, u32[]{:S(2)}) %collective-permute-start.4) | collective-permute-done | bytes 98336 | tf_op jit(solution)/shard_map/ppermute | solution.py:329
  39.0 4.3 %collective-permute-done.6.qb_ref = bf16[384,128]{1,0:T(8,128)(2,1)S(1)} collective-permute-done((bf16[384,128]{1,0:T(8,128)(2,1)S(1)}, bf16[384,128]{1,0:T(8,128)(2,1)S(1)}, u32[]{:S(2)}, u32[]{:S(2)}) %collective-permute-start.6) | collective-permute-done | bytes 98336 | tf_op jit(solution)/shard_map/ppermute | solution.py:329
  43.3 2.9 %all-to-all-done.came_ref = bf16[8,912,128]{2,1,0:T(8,128)(2,1)S(1)} async-done(((bf16[8,912,128]{2,1,0:T(8,128)(2,1)}), bf16[8,912,128]{2,1,0:T(8,128)(2,1)S(1)}, u32[]{:S(2)}, u32[]{:S(2)}) %all-to-all-start) | async-done | bytes 1867808 | tf_op jit(solution)/shard_map/all_to_all | solution.py:367
  46.2 1.6 %attention.4 = (bf16[432,128]{1,0:T(8,128)(2,1)S(1)}, bf16[432,128]{1,0:T(8,128)(2,1)S(1)}) custom-call(s32[3]{0:T(128)S(1)} %pad_add_fusion.scal_ref, s32[1]{0:T(128)S(6)} %copy.12.slot_ref, bf16[384,128]{1,0:T(8,128)(2,1)S(1)} %collective-permute-done.5.qa_ref, bf16[384,128]{1,0:T(8,128)(2,1)S(1)} %collective-permute-done.6.qb_ref, ...), custom_call_target="tpu_custom_call" | custom-call | tf_op jit(solution)/shard_map/attention/pallas_call | solution.py:226
  48.0 0.9 collective-permute-start.14
  48.9 0.4 collective-permute-start.15
  49.3 1.3 %collective-permute-start.16 = (bf16[384,640]{1,0:T(8,128)(2,1)S(1)}, bf16[384,640]{1,0:T(8,128)(2,1)S(1)}, u32[]{:S(2)}, u32[]{:S(2)}) collective-permute-start(bf16[384,640]{1,0:T(8,128)(2,1)S(1)} %get-tuple-element.70), channel_id=1, source_target_pairs={{0,3},{1,2},{2,1},{3,0},{4,7},{5,6},{6,5},{7,4},{8,11},{9,10},{10,... | collective-permute-start | bytes 1474568 | tf_op jit(solution)/shard_map/ppermute | solution.py:350
  50.6 1.6 %collective-permute-start.7 = (bf16[432,128]{1,0:T(8,128)(2,1)S(1)}, bf16[432,128]{1,0:T(8,128)(2,1)S(1)}, u32[]{:S(2)}, u32[]{:S(2)}) collective-permute-start(bf16[432,128]{1,0:T(8,128)(2,1)S(1)} %get-tuple-element.44), channel_id=1, source_target_pairs={{0,4},{4,8},{8,12},{12,16},{16,20},{20,24},{24,28},{28,0},{1,5},{5... | collective-permute-start | bytes 331784 | tf_op jit(solution)/shard_map/ppermute | solution.py:329
  52.2 3.9 %collective-permute-start.8 = (bf16[432,128]{1,0:T(8,128)(2,1)S(1)}, bf16[432,128]{1,0:T(8,128)(2,1)S(1)}, u32[]{:S(2)}, u32[]{:S(2)}) collective-permute-start(bf16[432,128]{1,0:T(8,128)(2,1)S(1)} %get-tuple-element.45), channel_id=1, source_target_pairs={{0,28},{4,0},{8,4},{12,8},{16,12},{20,16},{24,20},{28,24},{1,29},{... | collective-permute-start | bytes 331784 | tf_op jit(solution)/shard_map/ppermute | solution.py:329
  56.2 1.6 %attention.5 = (f32[432,128]{1,0:T(8,128)S(1)}, f32[432,128]{1,0:T(8,128)S(1)}) custom-call(s32[3]{0:T(128)S(1)} %pad_add_fusion.scal_ref, s32[1]{0:T(128)S(6)} %copy.12.slot_ref, bf16[384,128]{1,0:T(8,128)(2,1)S(1)} %collective-permute-done.3.qa_ref, bf16[384,128]{1,0:T(8,128)(2,1)S(1)} %collective-permute-done.4.qb_ref, ...), custom_call_target="tpu_custom_call" | custom-call | tf_op jit(solution)/shard_map/attention/pallas_call | solution.py:226
  57.7 1.7 %collective-permute-done.7.refs_0_ = bf16[432,128]{1,0:T(8,128)(2,1)S(1)} collective-permute-done((bf16[432,128]{1,0:T(8,128)(2,1)S(1)}, bf16[432,128]{1,0:T(8,128)(2,1)S(1)}, u32[]{:S(2)}, u32[]{:S(2)}) %collective-permute-start.7) | collective-permute-done | bytes 110624 | tf_op jit(solution)/shard_map/ppermute | solution.py:329
  59.6 2.7 %collective-permute-start.10 = (bf16[432,128]{1,0:T(8,128)(2,1)S(1)}, bf16[432,128]{1,0:T(8,128)(2,1)S(1)}, u32[]{:S(2)}, u32[]{:S(2)}) collective-permute-start(bf16[432,128]{1,0:T(8,128)(2,1)S(1)} %get-tuple-element.51), channel_id=1, source_target_pairs={{0,28},{4,0},{8,4},{12,8},{16,12},{20,16},{24,20},{28,24},{1,29},{... | collective-permute-start | bytes 331784 | tf_op jit(solution)/shard_map/ppermute | solution.py:329
  62.3 1.6 %attention.6 = (f32[432,128]{1,0:T(8,128)S(1)}, f32[432,128]{1,0:T(8,128)S(1)}) custom-call(s32[3]{0:T(128)S(1)} %pad_add_fusion.scal_ref, s32[1]{0:T(128)S(6)} %copy.12.slot_ref, bf16[384,128]{1,0:T(8,128)(2,1)S(1)} %collective-permute-done.1.qa_ref, bf16[384,128]{1,0:T(8,128)(2,1)S(1)} %collective-permute-done.2.qb_ref, ...), custom_call_target="tpu_custom_call" | custom-call | tf_op jit(solution)/shard_map/attention/pallas_call | solution.py:226
  63.8 0.6 collective-permute-done.9.refs_0_
  64.5 2.7 %collective-permute-start.12 = (bf16[432,128]{1,0:T(8,128)(2,1)S(1)}, bf16[432,128]{1,0:T(8,128)(2,1)S(1)}, u32[]{:S(2)}, u32[]{:S(2)}) collective-permute-start(bf16[432,128]{1,0:T(8,128)(2,1)S(1)} %get-tuple-element.57), channel_id=1, source_target_pairs={{0,28},{4,0},{8,4},{12,8},{16,12},{20,16},{24,20},{28,24},{1,29},{... | collective-permute-start | bytes 331784 | tf_op jit(solution)/shard_map/ppermute | solution.py:329
  67.2 1.6 %attention.7 = (f32[432,128]{1,0:T(8,128)S(1)}, f32[432,128]{1,0:T(8,128)S(1)}) custom-call(s32[3]{0:T(128)S(1)} %pad_add_fusion.scal_ref, s32[1]{0:T(128)S(6)} %copy.12.slot_ref, bf16[384,128]{1,0:T(8,128)(2,1)S(1)} %get-tuple-element.58.qa_ref, bf16[384,128]{1,0:T(8,128)(2,1)S(1)} %collective-permute-done.qb_ref, ...), custom_call_target="tpu_custom_call" | custom-call | tf_op jit(solution)/shard_map/attention/pallas_call | solution.py:226
  69.0 3.1 %collective-permute-start.13 = (bf16[432,128]{1,0:T(8,128)(2,1)S(1)}, bf16[432,128]{1,0:T(8,128)(2,1)S(1)}, u32[]{:S(2)}, u32[]{:S(2)}) collective-permute-start(bf16[432,128]{1,0:T(8,128)(2,1)S(1)} %joined.5), channel_id=1, source_target_pairs={{0,28},{4,0},{8,4},{12,8},{16,12},{20,16},{24,20},{28,24},{1,29},{... | collective-permute-start | bytes 331784 | tf_op jit(solution)/shard_map/ppermute | solution.py:329
  72.4 1.3 %collective-permute-done.11.up_ref = bf16[432,128]{1,0:T(8,128)(2,1)S(1)} collective-permute-done((bf16[432,128]{1,0:T(8,128)(2,1)S(1)}, bf16[432,128]{1,0:T(8,128)(2,1)S(1)}, u32[]{:S(2)}, u32[]{:S(2)}) %collective-permute-start.11) | collective-permute-done | bytes 110624 | tf_op jit(solution)/shard_map/ppermute | solution.py:329
  74.1 10.3 %all-gather.1 = bf16[576,384]{1,0:T(8,128)(2,1)S(1)} all-gather(bf16[144,384]{1,0:T(8,128)(2,1)S(1)} %get-tuple-element.64), channel_id=3, replica_groups=mesh['yh'=2,'x'=4,'z'=8,'yl'=2,'core'=2] {'yl','core'}, dimensions={0}, use_global_device_ids=true | all-gather | bytes 552960 | tf_op jit(solution)/shard_map/all_gather | solution.py:381
  84.4 1.8 %finish.1 = (bf16[128,640]{1,0:T(8,128)(2,1)}, bf16[2,640]{1,0:T(2,128)(2,1)}) custom-call(s32[3]{0:T(128)S(1)} %pad_add_fusion.scal_ref, s32[1]{0:T(128)S(6)} %copy.12.slot_ref, bf16[4,144,384]{2,1,0:T(8,128)(2,1)S(1)} %bitcast.12, bf16[384,640]{1,0:T(8,128)(2,1)S(1)} %get-tuple-element.65.w0_ref, bf16[384,640]{1,0:T(8,128)(2,1)S(1)} %collective-permute-done.14.w1_ref, ...), custom_call_target="tpu_custom_call" | custom-call | tf_op jit(solution)/shard_map/finish/pallas_call | solution.py:312
  (39 shorter events, 1.6 us)
Async XLA Ops:
  1.3 1.2 %copy-start.2 = (bf16[256,3,640]{2,0,1:T(8,128)(2,1)S(1)}, bf16[256,3,640]{2,0,1:T(8,128)(2,1)}, u32[]{:S(2)}) copy-start(bf16[256,3,640]{2,0,1:T(8,128)(2,1)} %param.13) | copy-start | bytes 2949124
  1.3 1.4 %copy-start.3 = (bf16[128,2560]{1,0:T(8,128)(2,1)S(1)}, bf16[128,2560]{1,0:T(8,128)(2,1)}, u32[]{:S(2)}) copy-start(bf16[128,2560]{1,0:T(8,128)(2,1)} %lat_ref.1) | copy-start | bytes 1966084
  1.3 1.4 %copy-start.4 = (f32[128]{0:T(128)S(1)}, f32[128]{0:T(128)}, u32[]{:S(2)}) copy-start(f32[128]{0:T(128)} %param.15) | copy-start | bytes 1540
  1.3 1.4 %copy-start.5 = (f32[128]{0:T(128)S(1)}, f32[128]{0:T(128)}, u32[]{:S(2)}) copy-start(f32[128]{0:T(128)} %param.16) | copy-start | bytes 1540
  1.5 10.6 %slice-start = ((s8[5898240]{0:T(1024)(128)(4,1)}), s8[4194304]{0:T(1024)(128)(4,1)S(1)}, s32[]{:S(2)}) async-start(s8[5898240]{0:T(1024)(128)(4,1)} %bitcast.9), calls=%async_computation.1 | async-start | bytes 8388608
  2.7 9.4 %slice-start.1 = ((s8[5898240]{0:T(1024)(128)(4,1)}), s8[1703936]{0:T(1024)(128)(4,1)S(1)}, s32[]{:S(2)}) async-start(s8[5898240]{0:T(1024)(128)(4,1)} %bitcast.9), calls=%async_computation.2 | async-start | bytes 3407872
  13.9 1.3 %copy-start = (bf16[8,912,128]{2,1,0:T(8,128)(2,1)}, bf16[8,912,128]{2,1,0:T(8,128)(2,1)S(1)}, u32[]{:S(2)}) copy-start(bf16[8,912,128]{2,1,0:T(8,128)(2,1)S(1)} %get-tuple-element.39) | copy-start | bytes 5603332
  15.2 31.1 %all-to-all-start = ((bf16[8,912,128]{2,1,0:T(8,128)(2,1)}), bf16[8,912,128]{2,1,0:T(8,128)(2,1)S(1)}, u32[]{:S(2)}, u32[]{:S(2)}) async-start(bf16[8,912,128]{2,1,0:T(8,128)(2,1)} %copy-done), calls=%async_computation | async-start | bytes 3735552 | tf_op jit(solution)/shard_map/all_to_all | solution.py:367
  20.1 8.3 %collective-permute-start = (bf16[384,128]{1,0:T(8,128)(2,1)S(1)}, bf16[384,128]{1,0:T(8,128)(2,1)S(1)}, u32[]{:S(2)}, u32[]{:S(2)}) collective-permute-start(bf16[384,128]{1,0:T(8,128)(2,1)S(1)} %get-tuple-element.58.qa_ref), channel_id=1, source_target_pairs={{0,4},{4,8},{8,12},{12,16},{16,20},{20,24},{24,28},{28,0},{1,5},{5... | collective-permute-start | bytes 294920 | tf_op jit(solution)/shard_map/ppermute | solution.py:329
  21.7 6.7 %collective-permute-start.1 = (bf16[384,128]{1,0:T(8,128)(2,1)S(1)}, bf16[384,128]{1,0:T(8,128)(2,1)S(1)}, u32[]{:S(2)}, u32[]{:S(2)}) collective-permute-start(bf16[384,128]{1,0:T(8,128)(2,1)S(1)} %get-tuple-element.58.qa_ref), channel_id=1, source_target_pairs={{0,28},{4,0},{8,4},{12,8},{16,12},{20,16},{24,20},{28,24},{1,29},{... | collective-permute-start | bytes 294920 | tf_op jit(solution)/shard_map/ppermute | solution.py:329
  28.4 5.0 %collective-permute-start.2 = (bf16[384,128]{1,0:T(8,128)(2,1)S(1)}, bf16[384,128]{1,0:T(8,128)(2,1)S(1)}, u32[]{:S(2)}, u32[]{:S(2)}) collective-permute-start(bf16[384,128]{1,0:T(8,128)(2,1)S(1)} %collective-permute-done.qb_ref), channel_id=1, source_target_pairs={{0,4},{4,8},{8,12},{12,16},{16,20},{20,24},{24,28},{28,0},{1,5},{5... | collective-permute-start | bytes 294920 | tf_op jit(solution)/shard_map/ppermute | solution.py:329
  28.4 5.0 %collective-permute-start.3 = (bf16[384,128]{1,0:T(8,128)(2,1)S(1)}, bf16[384,128]{1,0:T(8,128)(2,1)S(1)}, u32[]{:S(2)}, u32[]{:S(2)}) collective-permute-start(bf16[384,128]{1,0:T(8,128)(2,1)S(1)} %collective-permute-done.1.qa_ref), channel_id=1, source_target_pairs={{0,28},{4,0},{8,4},{12,8},{16,12},{20,16},{24,20},{28,24},{1,29},{... | collective-permute-start | bytes 294920 | tf_op jit(solution)/shard_map/ppermute | solution.py:329
  33.4 5.0 %collective-permute-start.4 = (bf16[384,128]{1,0:T(8,128)(2,1)S(1)}, bf16[384,128]{1,0:T(8,128)(2,1)S(1)}, u32[]{:S(2)}, u32[]{:S(2)}) collective-permute-start(bf16[384,128]{1,0:T(8,128)(2,1)S(1)} %collective-permute-done.2.qb_ref), channel_id=1, source_target_pairs={{0,4},{4,8},{8,12},{12,16},{16,20},{20,24},{24,28},{28,0},{1,5},{5... | collective-permute-start | bytes 294920 | tf_op jit(solution)/shard_map/ppermute | solution.py:329
  33.4 5.6 %collective-permute-start.5 = (bf16[384,128]{1,0:T(8,128)(2,1)S(1)}, bf16[384,128]{1,0:T(8,128)(2,1)S(1)}, u32[]{:S(2)}, u32[]{:S(2)}) collective-permute-start(bf16[384,128]{1,0:T(8,128)(2,1)S(1)} %collective-permute-done.3.qa_ref), channel_id=1, source_target_pairs={{0,28},{4,0},{8,4},{12,8},{16,12},{20,16},{24,20},{28,24},{1,29},{... | collective-permute-start | bytes 294920 | tf_op jit(solution)/shard_map/ppermute | solution.py:329
  38.4 5.0 %collective-permute-start.6 = (bf16[384,128]{1,0:T(8,128)(2,1)S(1)}, bf16[384,128]{1,0:T(8,128)(2,1)S(1)}, u32[]{:S(2)}, u32[]{:S(2)}) collective-permute-start(bf16[384,128]{1,0:T(8,128)(2,1)S(1)} %collective-permute-done.4.qb_ref), channel_id=1, source_target_pairs={{0,4},{4,8},{8,12},{12,16},{16,20},{20,24},{24,28},{28,0},{1,5},{5... | collective-permute-start | bytes 294920 | tf_op jit(solution)/shard_map/ppermute | solution.py:329
  46.2 1.6 %copy-start.6 = (bf16[384,2560]{1,0:T(8,128)(2,1)S(1)}, bf16[384,2560]{1,0:T(8,128)(2,1)}, u32[]{:S(2)}) copy-start(bf16[384,2560]{1,0:T(8,128)(2,1)} %param.17) | copy-start | bytes 5898244
  48.0 24.1 %collective-permute-start.14 = (bf16[384,640]{1,0:T(8,128)(2,1)S(1)}, bf16[384,640]{1,0:T(8,128)(2,1)S(1)}, u32[]{:S(2)}, u32[]{:S(2)}) collective-permute-start(bf16[384,640]{1,0:T(8,128)(2,1)S(1)} %get-tuple-element.72), channel_id=1, source_target_pairs={{0,1},{1,0},{2,3},{3,2},{4,5},{5,4},{6,7},{7,6},{8,9},{9,8},{10,11... | collective-permute-start | bytes 1474568 | tf_op jit(solution)/shard_map/ppermute | solution.py:350
  48.9 23.3 %collective-permute-start.15 = (bf16[384,640]{1,0:T(8,128)(2,1)S(1)}, bf16[384,640]{1,0:T(8,128)(2,1)S(1)}, u32[]{:S(2)}, u32[]{:S(2)}) collective-permute-start(bf16[384,640]{1,0:T(8,128)(2,1)S(1)} %get-tuple-element.71), channel_id=1, source_target_pairs={{0,2},{1,3},{2,0},{3,1},{4,6},{5,7},{6,4},{7,5},{8,10},{9,11},{10,... | collective-permute-start | bytes 1474568 | tf_op jit(solution)/shard_map/ppermute | solution.py:350
  49.3 23.1 %collective-permute-start.16 = (bf16[384,640]{1,0:T(8,128)(2,1)S(1)}, bf16[384,640]{1,0:T(8,128)(2,1)S(1)}, u32[]{:S(2)}, u32[]{:S(2)}) collective-permute-start(bf16[384,640]{1,0:T(8,128)(2,1)S(1)} %get-tuple-element.70), channel_id=1, source_target_pairs={{0,3},{1,2},{2,1},{3,0},{4,7},{5,6},{6,5},{7,4},{8,11},{9,10},{10,... | collective-permute-start | bytes 1474568 | tf_op jit(solution)/shard_map/ppermute | solution.py:350
  50.6 8.9 %collective-permute-start.7 = (bf16[432,128]{1,0:T(8,128)(2,1)S(1)}, bf16[432,128]{1,0:T(8,128)(2,1)S(1)}, u32[]{:S(2)}, u32[]{:S(2)}) collective-permute-start(bf16[432,128]{1,0:T(8,128)(2,1)S(1)} %get-tuple-element.44), channel_id=1, source_target_pairs={{0,4},{4,8},{8,12},{12,16},{16,20},{20,24},{24,28},{28,0},{1,5},{5... | collective-permute-start | bytes 331784 | tf_op jit(solution)/shard_map/ppermute | solution.py:329
  52.2 7.2 %collective-permute-start.8 = (bf16[432,128]{1,0:T(8,128)(2,1)S(1)}, bf16[432,128]{1,0:T(8,128)(2,1)S(1)}, u32[]{:S(2)}, u32[]{:S(2)}) collective-permute-start(bf16[432,128]{1,0:T(8,128)(2,1)S(1)} %get-tuple-element.45), channel_id=1, source_target_pairs={{0,28},{4,0},{8,4},{12,8},{16,12},{20,16},{24,20},{28,24},{1,29},{... | collective-permute-start | bytes 331784 | tf_op jit(solution)/shard_map/ppermute | solution.py:329
  59.5 4.9 %collective-permute-start.9 = (bf16[432,128]{1,0:T(8,128)(2,1)S(1)}, bf16[432,128]{1,0:T(8,128)(2,1)S(1)}, u32[]{:S(2)}, u32[]{:S(2)}) collective-permute-start(bf16[432,128]{1,0:T(8,128)(2,1)S(1)} %get-tuple-element.50), channel_id=1, source_target_pairs={{0,4},{4,8},{8,12},{12,16},{16,20},{20,24},{24,28},{28,0},{1,5},{5... | collective-permute-start | bytes 331784 | tf_op jit(solution)/shard_map/ppermute | solution.py:329
  59.6 4.8 %collective-permute-start.10 = (bf16[432,128]{1,0:T(8,128)(2,1)S(1)}, bf16[432,128]{1,0:T(8,128)(2,1)S(1)}, u32[]{:S(2)}, u32[]{:S(2)}) collective-permute-start(bf16[432,128]{1,0:T(8,128)(2,1)S(1)} %get-tuple-element.51), channel_id=1, source_target_pairs={{0,28},{4,0},{8,4},{12,8},{16,12},{20,16},{24,20},{28,24},{1,29},{... | collective-permute-start | bytes 331784 | tf_op jit(solution)/shard_map/ppermute | solution.py:329
  64.5 4.5 %collective-permute-start.12 = (bf16[432,128]{1,0:T(8,128)(2,1)S(1)}, bf16[432,128]{1,0:T(8,128)(2,1)S(1)}, u32[]{:S(2)}, u32[]{:S(2)}) collective-permute-start(bf16[432,128]{1,0:T(8,128)(2,1)S(1)} %get-tuple-element.57), channel_id=1, source_target_pairs={{0,28},{4,0},{8,4},{12,8},{16,12},{20,16},{24,20},{28,24},{1,29},{... | collective-permute-start | bytes 331784 | tf_op jit(solution)/shard_map/ppermute | solution.py:329
  68.8 4.9 %collective-permute-start.11 = (bf16[432,128]{1,0:T(8,128)(2,1)S(1)}, bf16[432,128]{1,0:T(8,128)(2,1)S(1)}, u32[]{:S(2)}, u32[]{:S(2)}) collective-permute-start(bf16[432,128]{1,0:T(8,128)(2,1)S(1)} %get-tuple-element.56), channel_id=1, source_target_pairs={{0,4},{4,8},{8,12},{12,16},{16,20},{20,24},{24,28},{28,0},{1,5},{5... | collective-permute-start | bytes 331784 | tf_op jit(solution)/shard_map/ppermute | solution.py:329
  69.0 4.9 %collective-permute-start.13 = (bf16[432,128]{1,0:T(8,128)(2,1)S(1)}, bf16[432,128]{1,0:T(8,128)(2,1)S(1)}, u32[]{:S(2)}, u32[]{:S(2)}) collective-permute-start(bf16[432,128]{1,0:T(8,128)(2,1)S(1)} %joined.5), channel_id=1, source_target_pairs={{0,28},{4,0},{8,4},{12,8},{16,12},{20,16},{24,20},{28,24},{1,29},{... | collective-permute-start | bytes 331784 | tf_op jit(solution)/shard_map/ppermute | solution.py:329
  72.4 12.0 %copy-start.1 = (bf16[128,640]{1,0:T(8,128)(2,1)S(1)}, bf16[128,640]{1,0:T(8,128)(2,1)}, u32[]{:S(2)}) copy-start(bf16[128,640]{1,0:T(8,128)(2,1)} %fresh_ref.1) | copy-start | bytes 491524
